TPU v7x, 32 devices: a whole 2x2x4 slice. The times are simulated.
32 devices in a mesh: prow: 4 (over z), pcol: 8 (over y, x, core).
Axes of the slice: x: 2, y: 2, z: 4, core: 2. Of those that a mesh axis runs over, the one named last changes fastest.
Arguments:
- matrix: float32 [2, 4, 256, 8, 256], P(None, 'prow', None, 'pcol'), may hold values from -6 to 6, as said below
Outputs:
- factored: float32 [2, 4, 256, 8, 256], P(None, 'prow', None, 'pcol')
Inputs may be any that keep to these rules, and one draw needn't show every extreme that they name: `matrix`: in the first 3 diagonal blocks every diagonal entry lies between 1.3 and 3.2, and diag(1/d) times the off-diagonal part of each such block has spectral norm below about 0.7.
All inputs are finite; a program needn't handle non-finite values.
Results may differ from a plain program's by a relative error of at most 0.0001.
Values sent between devices are 32-bit elements; how exact they have to be, the bound alone decides.
No kernel may reach another device: no remote copies, remote signals or barrier semaphores. Data moves between devices by JAX's collectives and lax.ppermute only.
A program may use at most 64 MiB of HBM per device.

v0:
```python
import functools
import math

import jax
import jax.numpy as jnp
from jax import lax
from jax.experimental import pallas as pl
from jax.experimental.pallas import tpu as pltpu
from jax.sharding import PartitionSpec as P


PANELS = 3


def split(value):
    high = value.astype(jnp.bfloat16)
    low = (value - high.astype(jnp.float32)).astype(jnp.bfloat16)
    return high, low


def product(left, right):
    dot = functools.partial(jnp.dot, preferred_element_type=jnp.float32)
    return dot(left[0], right[0]) + (dot(left[0], right[1]) + dot(left[1], right[0]))


def invert(block):
    size = block.shape[0]
    eye = lax.broadcasted_iota(jnp.int32, (size, size), 0) == lax.broadcasted_iota(jnp.int32, (size, size), 1)
    diagonal = jnp.where(eye, block, 0.0)
    down = 1.0 / jnp.sum(diagonal, axis=1, keepdims=True)
    along = 1.0 / jnp.sum(diagonal, axis=0, keepdims=True)
    first = jnp.where(eye, 2.0 * down, 0.0) - down * block * along
    parts = split(first)
    inner = product(split(block), parts)
    return 2.0 * first - product(parts, split(inner))


def distance_groups(row_count):
    groups = []
    for distance in range(1, row_count):
        targets = {(k + distance) % row_count for k in range(PANELS)}
        for group in groups:
            if not targets & group[1]:
                group[0].append(distance)
                group[1].update(targets)
                break
        else:
            groups.append(([distance], targets))
    groups = [group[0] for group in groups]
    return groups[:1] + groups[2:], groups[1]


LANES = 128


def load(ref, index, size):
    step = size // LANES
    return jnp.concatenate([ref[(*index, pl.ds(part, size, stride=step), slice(None))] for part in range(step)], axis=1)


def store(ref, index, value):
    size = value.shape[0]
    step = size // LANES
    for part in range(step):
        ref[(*index, pl.ds(part, size, stride=step), slice(None))] = value[:, part * LANES : (part + 1) * LANES]


def factor_kernel(size, tile, near, far, own_mine, own_other, far_mine, far_other, near_mine, near_other, out, work):
    count = tile.shape[0]
    row_count = lax.axis_size("prow")
    my_row = lax.axis_index("prow")
    my_col = lax.axis_index("pcol")
    even = lax.rem(my_col, 2) == 0

    def column(index):
        return slice(index * size, (index + 1) * size)

    def place(target, mine, other, piece, own, own_index):
        work[target, :, column(PANELS)] = load(own, (own_index,), size)

        @pl.when(even)
        def _():
            work[target, :, column(0)] = load(mine, (0, piece), size)
            work[target, :, column(1)] = load(other, (0, piece), size)
            work[target, :, column(2)] = load(mine, (1, piece), size)

        @pl.when(jnp.logical_not(even))
        def _():
            work[target, :, column(0)] = load(other, (0, piece), size)
            work[target, :, column(1)] = load(mine, (0, piece), size)
            work[target, :, column(2)] = load(other, (1, piece), size)

    for index in range(count):
        place(PANELS + index, own_mine, own_other, index, tile, index)

    @pl.when(my_row < PANELS)
    def _():
        place(my_row, own_mine, own_other, 0, tile, 0)

    far_groups, near_group = distance_groups(row_count)
    for number, group in enumerate([near_group] + far_groups):
        for distance in group:
            source = lax.rem(my_row + row_count - distance, row_count)

            @pl.when(source < PANELS)
            def _():
                if number == 0:
                    place(source, near_mine, near_other, 0, near, 0)
                else:
                    place(source, far_mine, far_other, number - 1, far, number - 1)

    for panel in range(PANELS):
        inverse = invert(work[panel, :, column(panel)])
        work[panel, :, column(panel)] = inverse
        inverse = split(inverse)
        rest = slice((panel + 1) * size, (PANELS + 1) * size)
        pivot_row = split(work[panel, :, rest])
        for index in range(panel + 1, PANELS + count):
            factor = product(split(work[index, :, column(panel)]), inverse)
            work[index, :, column(panel)] = factor
            work[index, :, rest] = work[index, :, rest] - product(split(factor), pivot_row)

    at = jnp.where(my_col < PANELS, my_col, PANELS)
    columns = pl.ds(pl.multiple_of(at * size, size), size)
    first = jnp.where(my_row < PANELS, my_row, PANELS)
    store(out, (0,), work[first, :, columns])
    for index in range(1, count):
        store(out, (index,), work[PANELS + index, :, columns])


def in_vmem(kernel, out_shape, operands, scratch=(), spare=4):
    words = sum(operand.size for operand in operands) + math.prod(out_shape) + sum(math.prod(s.shape) for s in scratch)
    return pl.pallas_call(
        kernel,
        out_shape=jax.ShapeDtypeStruct(out_shape, jnp.float32),
        in_specs=[pl.BlockSpec(memory_space=pltpu.VMEM)] * len(operands),
        out_specs=pl.BlockSpec(memory_space=pltpu.VMEM),
        scratch_shapes=list(scratch),
        compiler_params=pltpu.CompilerParams(vmem_limit_bytes=4 * words + spare * 1024 * 1024),
    )(*operands)


def factor(operands, size):
    count = operands[0].shape[0]
    work = pltpu.VMEM((PANELS + count, size, (PANELS + 1) * size), jnp.float32)
    return in_vmem(functools.partial(factor_kernel, size), operands[0].shape, operands, [work], 16)


def pick_kernel(*refs):
    sources, mine = refs[:-1], refs[-1]
    chip = lax.axis_index("pcol") // 2
    for index, source in enumerate(sources):
        for slot in range(2):

            @pl.when(chip == (index ^ slot))
            def _():
                mine[slot] = source[...]


def arrivals(block):
    arrived = {0: block}
    for mask in range(2, lax.axis_size("pcol"), 2):
        before = mask & (mask - 1)
        arrived[mask] = lax.ppermute(arrived[before], "pcol", [(c ^ before, c ^ mask) for c in range(PANELS)])
    return [arrived[mask] for mask in sorted(arrived)]


def exchange(arrived):
    mine = in_vmem(pick_kernel, (2, *arrived[0].shape), arrived)
    other = lax.ppermute(mine, "pcol", [(c, c ^ 1) for c in range(lax.axis_size("pcol"))])
    return mine, other


def factored(matrix):
    shape = matrix.shape
    size = shape[4]
    tile = matrix.reshape(shape[0], shape[2] * size // LANES, LANES)
    row_count = lax.axis_size("prow")
    far_groups, near_group = distance_groups(row_count)

    def from_rows(block, group):
        total = None
        for d in group:
            arrived = lax.ppermute(block, "prow", [(k, (k + d) % row_count) for k in range(PANELS)])
            total = arrived if total is None else total + arrived
        return total

    rows = [from_rows(tile[:1], group) for group in far_groups]
    own = arrivals(tile)
    late, first = lax.optimization_barrier((tile[:1], rows[0]))
    near = from_rows(late, near_group)
    far = jnp.concatenate([first] + rows[1:])
    operands = (tile, near, far, *exchange(own), *exchange(arrivals(far)), *exchange(arrivals(near)))
    return factor(operands, size).reshape(shape)


def solution(mesh):
    return jax.shard_map(
        factored,
        mesh=mesh,
        in_specs=(P(None, "prow", None, "pcol", None),),
        out_specs=P(None, "prow", None, "pcol", None),
        check_vma=False,
    )
```

profile of v0, /device:TPU:29, one launch (start us, length us, event | category | flops | bytes accessed | tf_op | source)
XLA Modules:
  0.0 72.7 jit_solution(7406973217581182881)
XLA Ops:
  0.0 0.0 copy-start
  0.0 1.2 %slice.8 = f32[1,1,256,1,256]{4,3,2,1,0:T(1,128)S(1)} slice(f32[2,1,256,1,256]{4,3,2,1,0:T(1,128)} %param.1), slice={[0:1], [0:1], [0:256], [0:1], [0:256]} | slice | bytes 524288 | tf_op jit(solution)/shard_map/slice | solution.py:190
  1.2 1.3 %collective-permute-start = (f32[1,512,128]{2,1,0:T(8,128)S(1)}, f32[1,512,128]{2,1,0:T(8,128)S(1)}, u32[]{:S(2)}, u32[]{:S(2)}) collective-permute-start(f32[1,512,128]{2,1,0:T(8,128)S(1)} %bitcast.7), channel_id=1, source_target_pairs={{0,8},{8,16},{16,24},{1,9},{9,17},{17,25},{2,10},{10,18},{18,26},{... | collective-permute-start | bytes 786440 | tf_op jit(solution)/shard_map/ppermute | solution.py:184
  2.5 1.3 %collective-permute-start.2 = (f32[1,512,128]{2,1,0:T(8,128)S(1)}, f32[1,512,128]{2,1,0:T(8,128)S(1)}, u32[]{:S(2)}, u32[]{:S(2)}) collective-permute-start(f32[1,512,128]{2,1,0:T(8,128)S(1)} %bitcast.8), channel_id=1, source_target_pairs={{0,24},{8,0},{16,8},{1,25},{9,1},{17,9},{2,26},{10,2},{18,10},{3,2... | collective-permute-start | bytes 786440 | tf_op jit(solution)/shard_map/ppermute | solution.py:184
  3.8 0.0 copy-done
  3.8 1.3 %collective-permute-start.4 = (f32[2,512,128]{2,1,0:T(8,128)S(1)}, f32[2,512,128]{2,1,0:T(8,128)S(1)}, u32[]{:S(2)}, u32[]{:S(2)}) collective-permute-start(f32[2,512,128]{2,1,0:T(8,128)S(1)} %bitcast.3), channel_id=1, source_target_pairs={{0,4},{1,5},{2,6},{8,12},{9,13},{10,14},{16,20},{17,21},{18,22},{2... | collective-permute-start | bytes 1572872 | tf_op jit(solution)/shard_map/ppermute | solution.py:164
  5.1 5.4 %collective-permute-done = f32[1,512,128]{2,1,0:T(8,128)S(1)} collective-permute-done((f32[1,512,128]{2,1,0:T(8,128)S(1)}, f32[1,512,128]{2,1,0:T(8,128)S(1)}, u32[]{:S(2)}, u32[]{:S(2)}) %collective-permute-start) | collective-permute-done | bytes 262176 | tf_op jit(solution)/shard_map/ppermute | solution.py:184
  10.5 5.2 %collective-permute-done.2 = f32[1,512,128]{2,1,0:T(8,128)S(1)} collective-permute-done((f32[1,512,128]{2,1,0:T(8,128)S(1)}, f32[1,512,128]{2,1,0:T(8,128)S(1)}, u32[]{:S(2)}, u32[]{:S(2)}) %collective-permute-start.2) | collective-permute-done | bytes 262176 | tf_op jit(solution)/shard_map/ppermute | solution.py:184
  15.8 1.3 %collective-permute-start.8 = (f32[2,512,128]{2,1,0:T(8,128)S(1)}, f32[2,512,128]{2,1,0:T(8,128)S(1)}, u32[]{:S(2)}, u32[]{:S(2)}) collective-permute-start(f32[2,512,128]{2,1,0:T(8,128)S(1)} %constant_dynamic-update-slice_fusion.refs_0_.far), channel_id=1, source_target_pairs={{0,4},{1,5},{2,6},{8,12},{9,13},{10,14},{16,20},{17,21},{18,22},{2... | collective-permute-start | bytes 1572872 | tf_op jit(solution)/shard_map/ppermute | solution.py:164
  17.1 0.7 collective-permute-start.3
  17.8 0.8 %collective-permute-done.4.refs_2_ = f32[2,512,128]{2,1,0:T(8,128)S(1)} collective-permute-done((f32[2,512,128]{2,1,0:T(8,128)S(1)}, f32[2,512,128]{2,1,0:T(8,128)S(1)}, u32[]{:S(2)}, u32[]{:S(2)}) %collective-permute-start.4) | collective-permute-done | bytes 524320 | tf_op jit(solution)/shard_map/ppermute | solution.py:164
  18.5 1.8 %collective-permute-start.5 = (f32[2,512,128]{2,1,0:T(8,128)S(1)}, f32[2,512,128]{2,1,0:T(8,128)S(1)}, u32[]{:S(2)}, u32[]{:S(2)}) collective-permute-start(f32[2,512,128]{2,1,0:T(8,128)S(1)} %collective-permute-done.4.refs_2_), channel_id=1, source_target_pairs={{4,6},{5,7},{6,4},{12,14},{13,15},{14,12},{20,22},{21,23},{22,20},... | collective-permute-start | bytes 1572872 | tf_op jit(solution)/shard_map/ppermute | solution.py:164
  20.3 0.7 collective-permute-start.7
  21.0 8.4 %collective-permute-done.8.refs_2_ = f32[2,512,128]{2,1,0:T(8,128)S(1)} collective-permute-done((f32[2,512,128]{2,1,0:T(8,128)S(1)}, f32[2,512,128]{2,1,0:T(8,128)S(1)}, u32[]{:S(2)}, u32[]{:S(2)}) %collective-permute-start.8) | collective-permute-done | bytes 524320 | tf_op jit(solution)/shard_map/ppermute | solution.py:164
  29.4 1.3 %collective-permute-start.9 = (f32[2,512,128]{2,1,0:T(8,128)S(1)}, f32[2,512,128]{2,1,0:T(8,128)S(1)}, u32[]{:S(2)}, u32[]{:S(2)}) collective-permute-start(f32[2,512,128]{2,1,0:T(8,128)S(1)} %collective-permute-done.8.refs_2_), channel_id=1, source_target_pairs={{4,6},{5,7},{6,4},{12,14},{13,15},{14,12},{20,22},{21,23},{22,20},... | collective-permute-start | bytes 1572872 | tf_op jit(solution)/shard_map/ppermute | solution.py:164
  30.7 1.3 %collective-permute-start.1 = (f32[1,512,128]{2,1,0:T(8,128)S(1)}, f32[1,512,128]{2,1,0:T(8,128)S(1)}, u32[]{:S(2)}, u32[]{:S(2)}) collective-permute-start(f32[1,512,128]{2,1,0:T(8,128)S(1)} %bitcast.9), channel_id=1, source_target_pairs={{0,16},{8,24},{16,0},{1,17},{9,25},{17,1},{2,18},{10,26},{18,2},{3... | collective-permute-start | bytes 786440 | tf_op jit(solution)/shard_map/ppermute | solution.py:184
  32.0 12.9 %collective-permute-done.1.refs_0_.near = f32[1,512,128]{2,1,0:T(8,128)S(1)} collective-permute-done((f32[1,512,128]{2,1,0:T(8,128)S(1)}, f32[1,512,128]{2,1,0:T(8,128)S(1)}, u32[]{:S(2)}, u32[]{:S(2)}) %collective-permute-start.1) | collective-permute-done | bytes 262176 | tf_op jit(solution)/shard_map/ppermute | solution.py:184
  44.9 1.3 %collective-permute-start.12 = (f32[1,512,128]{2,1,0:T(8,128)S(1)}, f32[1,512,128]{2,1,0:T(8,128)S(1)}, u32[]{:S(2)}, u32[]{:S(2)}) collective-permute-start(f32[1,512,128]{2,1,0:T(8,128)S(1)} %collective-permute-done.1.refs_0_.near), channel_id=1, source_target_pairs={{0,4},{1,5},{2,6},{8,12},{9,13},{10,14},{16,20},{17,21},{18,22},{2... | collective-permute-start | bytes 786440 | tf_op jit(solution)/shard_map/ppermute | solution.py:164
  46.2 0.0 collective-permute-done.3.refs_1_
  46.2 0.0 collective-permute-done.5.refs_3_
  46.2 0.1 shard_map.17.own_mine
  46.3 3.0 %collective-permute-start.6 = (f32[2,2,512,128]{3,2,1,0:T(8,128)S(1)}, f32[2,2,512,128]{3,2,1,0:T(8,128)S(1)}, u32[]{:S(2)}, u32[]{:S(2)}) collective-permute-start(f32[2,2,512,128]{3,2,1,0:T(8,128)S(1)} %shard_map.17.own_mine), channel_id=1, source_target_pairs={{0,1},{1,0},{2,3},{3,2},{4,5},{5,4},{6,7},{7,6},{8,9},{9,8},{10,11... | collective-permute-start | bytes 3145736 | tf_op jit(solution)/shard_map/ppermute | solution.py:170
  49.3 0.0 collective-permute-done.7.refs_1_
  49.3 0.0 collective-permute-done.9.refs_3_
  49.3 0.1 shard_map.18.far_mine
  49.4 0.1 collective-permute-start.10
  49.5 0.7 collective-permute-start.11
  50.2 1.8 %collective-permute-done.12.refs_2_ = f32[1,512,128]{2,1,0:T(8,128)S(1)} collective-permute-done((f32[1,512,128]{2,1,0:T(8,128)S(1)}, f32[1,512,128]{2,1,0:T(8,128)S(1)}, u32[]{:S(2)}, u32[]{:S(2)}) %collective-permute-start.12) | collective-permute-done | bytes 262176 | tf_op jit(solution)/shard_map/ppermute | solution.py:164
  52.0 1.3 %collective-permute-start.13 = (f32[1,512,128]{2,1,0:T(8,128)S(1)}, f32[1,512,128]{2,1,0:T(8,128)S(1)}, u32[]{:S(2)}, u32[]{:S(2)}) collective-permute-start(f32[1,512,128]{2,1,0:T(8,128)S(1)} %collective-permute-done.12.refs_2_), channel_id=1, source_target_pairs={{4,6},{5,7},{6,4},{12,14},{13,15},{14,12},{20,22},{21,23},{22,20},... | collective-permute-start | bytes 786440 | tf_op jit(solution)/shard_map/ppermute | solution.py:164
  53.3 0.0 collective-permute-done.11.refs_1_
  53.3 3.3 %collective-permute-done.13.refs_3_ = f32[1,512,128]{2,1,0:T(8,128)S(1)} collective-permute-done((f32[1,512,128]{2,1,0:T(8,128)S(1)}, f32[1,512,128]{2,1,0:T(8,128)S(1)}, u32[]{:S(2)}, u32[]{:S(2)}) %collective-permute-start.13) | collective-permute-done | bytes 262176 | tf_op jit(solution)/shard_map/ppermute | solution.py:164
  56.7 7.8 %collective-permute-start.14 = (f32[2,1,512,128]{3,2,1,0:T(8,128)S(1)}, f32[2,1,512,128]{3,2,1,0:T(8,128)S(1)}, u32[]{:S(2)}, u32[]{:S(2)}) collective-permute-start(f32[2,1,512,128]{3,2,1,0:T(8,128)S(1)} %shard_map.19.near_mine), channel_id=1, source_target_pairs={{0,1},{1,0},{2,3},{3,2},{4,5},{5,4},{6,7},{7,6},{8,9},{9,8},{10,11... | collective-permute-start | bytes 1572872 | tf_op jit(solution)/shard_map/ppermute | solution.py:170
  64.5 1.5 %collective-permute-done.14.near_other = f32[2,1,512,128]{3,2,1,0:T(8,128)S(1)} collective-permute-done((f32[2,1,512,128]{3,2,1,0:T(8,128)S(1)}, f32[2,1,512,128]{3,2,1,0:T(8,128)S(1)}, u32[]{:S(2)}, u32[]{:S(2)}) %collective-permute-start.14) | collective-permute-done | bytes 524320 | tf_op jit(solution)/shard_map/ppermute | solution.py:170
  66.0 0.0 collective-permute-done.6.own_other
  66.0 0.0 collective-permute-done.10.far_other
  66.0 6.7 %shard_map.20 = f32[2,512,128]{2,1,0:T(8,128)} custom-call(f32[2,512,128]{2,1,0:T(8,128)S(1)} %bitcast.6, f32[1,512,128]{2,1,0:T(8,128)S(1)} %collective-permute-done.1.refs_0_.near, f32[2,512,128]{2,1,0:T(8,128)S(1)} %constant_dynamic-update-slice_fusion.refs_0_.far, f32[2,2,512,128]{3,2,1,0:T(8,128)S(1)} %shard_map.17.own_mine, ...), custom_call_target="tpu_custom_call" | custom-call | tf_op jit(solution)/shard_map/pallas_call | solution.py:133
  (3 shorter events, 0.1 us)
Async XLA Ops:
  0.0 3.8 %copy-start = (f32[2,1,256,1,256]{4,3,2,1,0:T(1,128)S(1)}, f32[2,1,256,1,256]{4,3,2,1,0:T(1,128)}, u32[]{:S(2)}) copy-start(f32[2,1,256,1,256]{4,3,2,1,0:T(1,128)} %param.1) | copy-start | bytes 1572868
  1.2 9.3 %collective-permute-start = (f32[1,512,128]{2,1,0:T(8,128)S(1)}, f32[1,512,128]{2,1,0:T(8,128)S(1)}, u32[]{:S(2)}, u32[]{:S(2)}) collective-permute-start(f32[1,512,128]{2,1,0:T(8,128)S(1)} %bitcast.7), channel_id=1, source_target_pairs={{0,8},{8,16},{16,24},{1,9},{9,17},{17,25},{2,10},{10,18},{18,26},{... | collective-permute-start | bytes 786440 | tf_op jit(solution)/shard_map/ppermute | solution.py:184
  2.5 13.2 %collective-permute-start.2 = (f32[1,512,128]{2,1,0:T(8,128)S(1)}, f32[1,512,128]{2,1,0:T(8,128)S(1)}, u32[]{:S(2)}, u32[]{:S(2)}) collective-permute-start(f32[1,512,128]{2,1,0:T(8,128)S(1)} %bitcast.8), channel_id=1, source_target_pairs={{0,24},{8,0},{16,8},{1,25},{9,1},{17,9},{2,26},{10,2},{18,10},{3,2... | collective-permute-start | bytes 786440 | tf_op jit(solution)/shard_map/ppermute | solution.py:184
  3.8 14.7 %collective-permute-start.4 = (f32[2,512,128]{2,1,0:T(8,128)S(1)}, f32[2,512,128]{2,1,0:T(8,128)S(1)}, u32[]{:S(2)}, u32[]{:S(2)}) collective-permute-start(f32[2,512,128]{2,1,0:T(8,128)S(1)} %bitcast.3), channel_id=1, source_target_pairs={{0,4},{1,5},{2,6},{8,12},{9,13},{10,14},{16,20},{17,21},{18,22},{2... | collective-permute-start | bytes 1572872 | tf_op jit(solution)/shard_map/ppermute | solution.py:164
  15.8 13.6 %collective-permute-start.8 = (f32[2,512,128]{2,1,0:T(8,128)S(1)}, f32[2,512,128]{2,1,0:T(8,128)S(1)}, u32[]{:S(2)}, u32[]{:S(2)}) collective-permute-start(f32[2,512,128]{2,1,0:T(8,128)S(1)} %constant_dynamic-update-slice_fusion.refs_0_.far), channel_id=1, source_target_pairs={{0,4},{1,5},{2,6},{8,12},{9,13},{10,14},{16,20},{17,21},{18,22},{2... | collective-permute-start | bytes 1572872 | tf_op jit(solution)/shard_map/ppermute | solution.py:164
  17.1 29.2 %collective-permute-start.3 = (f32[2,512,128]{2,1,0:T(8,128)S(1)}, f32[2,512,128]{2,1,0:T(8,128)S(1)}, u32[]{:S(2)}, u32[]{:S(2)}) collective-permute-start(f32[2,512,128]{2,1,0:T(8,128)S(1)} %bitcast.4), channel_id=1, source_target_pairs={{0,2},{1,3},{2,0},{8,10},{9,11},{10,8},{16,18},{17,19},{18,16},{24... | collective-permute-start | bytes 1572872 | tf_op jit(solution)/shard_map/ppermute | solution.py:164
  18.5 27.7 %collective-permute-start.5 = (f32[2,512,128]{2,1,0:T(8,128)S(1)}, f32[2,512,128]{2,1,0:T(8,128)S(1)}, u32[]{:S(2)}, u32[]{:S(2)}) collective-permute-start(f32[2,512,128]{2,1,0:T(8,128)S(1)} %collective-permute-done.4.refs_2_), channel_id=1, source_target_pairs={{4,6},{5,7},{6,4},{12,14},{13,15},{14,12},{20,22},{21,23},{22,20},... | collective-permute-start | bytes 1572872 | tf_op jit(solution)/shard_map/ppermute | solution.py:164
  20.3 29.0 %collective-permute-start.7 = (f32[2,512,128]{2,1,0:T(8,128)S(1)}, f32[2,512,128]{2,1,0:T(8,128)S(1)}, u32[]{:S(2)}, u32[]{:S(2)}) collective-permute-start(f32[2,512,128]{2,1,0:T(8,128)S(1)} %constant_dynamic-update-slice_fusion.refs_0_.far), channel_id=1, source_target_pairs={{0,2},{1,3},{2,0},{8,10},{9,11},{10,8},{16,18},{17,19},{18,16},{24... | collective-permute-start | bytes 1572872 | tf_op jit(solution)/shard_map/ppermute | solution.py:164
  29.4 19.9 %collective-permute-start.9 = (f32[2,512,128]{2,1,0:T(8,128)S(1)}, f32[2,512,128]{2,1,0:T(8,128)S(1)}, u32[]{:S(2)}, u32[]{:S(2)}) collective-permute-start(f32[2,512,128]{2,1,0:T(8,128)S(1)} %collective-permute-done.8.refs_2_), channel_id=1, source_target_pairs={{4,6},{5,7},{6,4},{12,14},{13,15},{14,12},{20,22},{21,23},{22,20},... | collective-permute-start | bytes 1572872 | tf_op jit(solution)/shard_map/ppermute | solution.py:164
  30.7 14.2 %collective-permute-start.1 = (f32[1,512,128]{2,1,0:T(8,128)S(1)}, f32[1,512,128]{2,1,0:T(8,128)S(1)}, u32[]{:S(2)}, u32[]{:S(2)}) collective-permute-start(f32[1,512,128]{2,1,0:T(8,128)S(1)} %bitcast.9), channel_id=1, source_target_pairs={{0,16},{8,24},{16,0},{1,17},{9,25},{17,1},{2,18},{10,26},{18,2},{3... | collective-permute-start | bytes 786440 | tf_op jit(solution)/shard_map/ppermute | solution.py:184
  44.9 7.1 %collective-permute-start.12 = (f32[1,512,128]{2,1,0:T(8,128)S(1)}, f32[1,512,128]{2,1,0:T(8,128)S(1)}, u32[]{:S(2)}, u32[]{:S(2)}) collective-permute-start(f32[1,512,128]{2,1,0:T(8,128)S(1)} %collective-permute-done.1.refs_0_.near), channel_id=1, source_target_pairs={{0,4},{1,5},{2,6},{8,12},{9,13},{10,14},{16,20},{17,21},{18,22},{2... | collective-permute-start | bytes 786440 | tf_op jit(solution)/shard_map/ppermute | solution.py:164
  46.3 19.6 %collective-permute-start.6 = (f32[2,2,512,128]{3,2,1,0:T(8,128)S(1)}, f32[2,2,512,128]{3,2,1,0:T(8,128)S(1)}, u32[]{:S(2)}, u32[]{:S(2)}) collective-permute-start(f32[2,2,512,128]{3,2,1,0:T(8,128)S(1)} %shard_map.17.own_mine), channel_id=1, source_target_pairs={{0,1},{1,0},{2,3},{3,2},{4,5},{5,4},{6,7},{7,6},{8,9},{9,8},{10,11... | collective-permute-start | bytes 3145736 | tf_op jit(solution)/shard_map/ppermute | solution.py:170
  49.4 16.6 %collective-permute-start.10 = (f32[2,2,512,128]{3,2,1,0:T(8,128)S(1)}, f32[2,2,512,128]{3,2,1,0:T(8,128)S(1)}, u32[]{:S(2)}, u32[]{:S(2)}) collective-permute-start(f32[2,2,512,128]{3,2,1,0:T(8,128)S(1)} %shard_map.18.far_mine), channel_id=1, source_target_pairs={{0,1},{1,0},{2,3},{3,2},{4,5},{5,4},{6,7},{7,6},{8,9},{9,8},{10,11... | collective-permute-start | bytes 3145736 | tf_op jit(solution)/shard_map/ppermute | solution.py:170
  49.5 3.8 %collective-permute-start.11 = (f32[1,512,128]{2,1,0:T(8,128)S(1)}, f32[1,512,128]{2,1,0:T(8,128)S(1)}, u32[]{:S(2)}, u32[]{:S(2)}) collective-permute-start(f32[1,512,128]{2,1,0:T(8,128)S(1)} %collective-permute-done.1.refs_0_.near), channel_id=1, source_target_pairs={{0,2},{1,3},{2,0},{8,10},{9,11},{10,8},{16,18},{17,19},{18,16},{24... | collective-permute-start | bytes 786440 | tf_op jit(solution)/shard_map/ppermute | solution.py:164
  52.0 4.6 %collective-permute-start.13 = (f32[1,512,128]{2,1,0:T(8,128)S(1)}, f32[1,512,128]{2,1,0:T(8,128)S(1)}, u32[]{:S(2)}, u32[]{:S(2)}) collective-permute-start(f32[1,512,128]{2,1,0:T(8,128)S(1)} %collective-permute-done.12.refs_2_), channel_id=1, source_target_pairs={{4,6},{5,7},{6,4},{12,14},{13,15},{14,12},{20,22},{21,23},{22,20},... | collective-permute-start | bytes 786440 | tf_op jit(solution)/shard_map/ppermute | solution.py:164
  56.7 9.3 %collective-permute-start.14 = (f32[2,1,512,128]{3,2,1,0:T(8,128)S(1)}, f32[2,1,512,128]{3,2,1,0:T(8,128)S(1)}, u32[]{:S(2)}, u32[]{:S(2)}) collective-permute-start(f32[2,1,512,128]{3,2,1,0:T(8,128)S(1)} %shard_map.19.near_mine), channel_id=1, source_target_pairs={{0,1},{1,0},{2,3},{3,2},{4,5},{5,4},{6,7},{7,6},{8,9},{9,8},{10,11... | collective-permute-start | bytes 1572872 | tf_op jit(solution)/shard_map/ppermute | solution.py:170
where the time goes:
time: 73.1 us; the launch traced here: 72.7 us
  waiting for transfers between devices  39.3 us (54%)
  starting transfers between devices  25.1 us (34%)
  Pallas kernels  6.93 us (9%)
  local copies, waits for them, and re-layouts  1.24 us (2%)
    ppermute x3, waiting for transfers between devices, from_rows(): lax.ppermute(block, 'prow', [(k, (k + d) % row_count) for k in range(PANE...  23.5 us
    ppermute x9, waiting for transfers between devices, arrivals(): lax.ppermute(arrived[before], 'pcol', [(c ^ before, c ^ mask) for c in ra...  14.2 us
    ppermute x3, starting transfers between devices, exchange(): lax.ppermute(mine, 'pcol', [(c, c ^ 1) for c in range(lax.axis_size('pcol...  10.9 us
    ppermute x9, starting transfers between devices, arrivals(): lax.ppermute(arrived[before], 'pcol', [(c ^ before, c ^ mask) for c in ra...  10.3 us
    pallas_call x4, Pallas kernels, in_vmem(): pl.pallas_call(kernel, out_shape=jax.ShapeDtypeStruct(out_shape, jnp.floa...  6.93 us
    ppermute x3, starting transfers between devices, from_rows(): lax.ppermute(block, 'prow', [(k, (k + d) % row_count) for k in range(PANE...  3.88 us
    ppermute x3, waiting for transfers between devices, exchange(): lax.ppermute(mine, 'pcol', [(c, c ^ 1) for c in range(lax.axis_size('pcol...  1.54 us
  transfers between devices with their start and end apart: 15, of which 8 were waited for; matrix products, arithmetic and copies ran while one was open for 0% of the time, Pallas kernels for 0%

commit v1 on v0

--- a/solution.py
+++ b/solution.py
@@ -146,23 +146,44 @@
     return in_vmem(functools.partial(factor_kernel, size), operands[0].shape, operands, [work], 16)
 
 
+def place_on_ring(position):
+    return position ^ (position >> 1)
+
+
+def ring_steps(chips):
+    steps = []
+    for step in range(chips - 1):
+        hops = ((step, step + 1, 0), (-step, -step - 1, 1), (1 - step, -step, 0))
+        steps.append(
+            [(2 * place_on_ring(a % chips) + core, 2 * place_on_ring(b % chips) + core) for a, b, core in hops]
+        )
+    return steps
+
+
 def pick_kernel(*refs):
     sources, mine = refs[:-1], refs[-1]
-    chip = lax.axis_index("pcol") // 2
-    for index, source in enumerate(sources):
-        for slot in range(2):
-
-            @pl.when(chip == (index ^ slot))
+    chips = len(sources)
+    me = lax.axis_index("pcol")
+    even = lax.rem(me, 2) == 0
+    for position in range(chips):
+
+        @pl.when(me // 2 == place_on_ring(position))
+        def _():
+            @pl.when(even)
             def _():
-                mine[slot] = source[...]
+                mine[0] = sources[position][...]
+                mine[1] = sources[(1 - position) % chips][...]
+
+            @pl.when(jnp.logical_not(even))
+            def _():
+                mine[0] = sources[-position % chips][...]
 
 
 def arrivals(block):
-    arrived = {0: block}
-    for mask in range(2, lax.axis_size("pcol"), 2):
-        before = mask & (mask - 1)
-        arrived[mask] = lax.ppermute(arrived[before], "pcol", [(c ^ before, c ^ mask) for c in range(PANELS)])
-    return [arrived[mask] for mask in sorted(arrived)]
+    arrived = [block]
+    for pairs in ring_steps(lax.axis_size("pcol") // 2):
+        arrived.append(lax.ppermute(arrived[-1], "pcol", pairs))
+    return arrived
 
 
 def exchange(arrived):

time: 73.1 us -> 73.5 us (level)
  starting transfers between devices: 25.1 us -> 31.4 us
  waiting for transfers between devices: 39.3 us -> 33.4 us
    ppermute x3, waiting for transfers between devices: 23.5 us -> 11.1 us  [from_rows(): lax.ppermute(block, 'prow', [(k, (k + d) % row_count) for k in range(PANE...]
    ppermute x9, waiting for transfers between devices: 14.2 us -> 20.8 us  [arrivals(): arrived.append(lax.ppermute(arrived[-1], 'pcol', pairs))]
    ppermute x3, starting transfers between devices: 10.9 us -> 16.5 us  [exchange(): lax.ppermute(mine, 'pcol', [(c, c ^ 1) for c in range(lax.axis_size('pcol...]
    ppermute x9, starting transfers between devices: 10.3 us -> 11.1 us  [arrivals(): arrived.append(lax.ppermute(arrived[-1], 'pcol', pairs))]
where the time goes in v1:
time: 73.5 us; the launch traced here: 73.2 us
  waiting for transfers between devices  33.4 us (45%)
  starting transfers between devices  31.4 us (43%)
  Pallas kernels  6.91 us (9%)
  local copies, waits for them, and re-layouts  1.24 us (2%)
    ppermute x9, waiting for transfers between devices, arrivals(): arrived.append(lax.ppermute(arrived[-1], 'pcol', pairs))  20.8 us
    ppermute x3, starting transfers between devices, exchange(): lax.ppermute(mine, 'pcol', [(c, c ^ 1) for c in range(lax.axis_size('pcol...  16.5 us
    ppermute x3, waiting for transfers between devices, from_rows(): lax.ppermute(block, 'prow', [(k, (k + d) % row_count) for k in range(PANE...  11.1 us
    ppermute x9, starting transfers between devices, arrivals(): arrived.append(lax.ppermute(arrived[-1], 'pcol', pairs))  11.1 us
    pallas_call x4, Pallas kernels, in_vmem(): pl.pallas_call(kernel, out_shape=jax.ShapeDtypeStruct(out_shape, jnp.floa...  6.91 us
    ppermute x3, starting transfers between devices, from_rows(): lax.ppermute(block, 'prow', [(k, (k + d) % row_count) for k in range(PANE...  3.88 us
    ppermute x3, waiting for transfers between devices, exchange(): lax.ppermute(mine, 'pcol', [(c, c ^ 1) for c in range(lax.axis_size('pcol...  1.54 us
  transfers between devices with their start and end apart: 15, of which 8 were waited for; matrix products, arithmetic and copies ran while one was open for 0% of the time, Pallas kernels for 0%

profile of v1, /device:TPU:29, one launch (start us, length us, event | category | flops | bytes accessed | tf_op | source)
XLA Modules:
  0.0 73.2 jit_solution(4134819271994084456)
XLA Ops:
  0.0 0.0 copy-start
  0.0 1.2 %slice.8 = f32[1,1,256,1,256]{4,3,2,1,0:T(1,128)S(1)} slice(f32[2,1,256,1,256]{4,3,2,1,0:T(1,128)} %param.1), slice={[0:1], [0:1], [0:256], [0:1], [0:256]} | slice | bytes 524288 | tf_op jit(solution)/shard_map/slice | solution.py:211
  1.2 1.3 %collective-permute-start = (f32[1,512,128]{2,1,0:T(8,128)S(1)}, f32[1,512,128]{2,1,0:T(8,128)S(1)}, u32[]{:S(2)}, u32[]{:S(2)}) collective-permute-start(f32[1,512,128]{2,1,0:T(8,128)S(1)} %bitcast.6), channel_id=1, source_target_pairs={{0,8},{8,16},{16,24},{1,9},{9,17},{17,25},{2,10},{10,18},{18,26},{... | collective-permute-start | bytes 786440 | tf_op jit(solution)/shard_map/ppermute | solution.py:205
  2.5 1.3 %collective-permute-start.2 = (f32[1,512,128]{2,1,0:T(8,128)S(1)}, f32[1,512,128]{2,1,0:T(8,128)S(1)}, u32[]{:S(2)}, u32[]{:S(2)}) collective-permute-start(f32[1,512,128]{2,1,0:T(8,128)S(1)} %bitcast.7), channel_id=1, source_target_pairs={{0,24},{8,0},{16,8},{1,25},{9,1},{17,9},{2,26},{10,2},{18,10},{3,2... | collective-permute-start | bytes 786440 | tf_op jit(solution)/shard_map/ppermute | solution.py:205
  3.8 0.0 copy-done
  3.8 1.3 %collective-permute-start.3 = (f32[2,512,128]{2,1,0:T(8,128)S(1)}, f32[2,512,128]{2,1,0:T(8,128)S(1)}, u32[]{:S(2)}, u32[]{:S(2)}) collective-permute-start(f32[2,512,128]{2,1,0:T(8,128)S(1)} %bitcast.3), channel_id=1, source_target_pairs={{0,2},{1,5},{2,0},{8,10},{9,13},{10,8},{16,18},{17,21},{18,16},{24... | collective-permute-start | bytes 1572872 | tf_op jit(solution)/shard_map/ppermute | solution.py:185
  5.1 5.4 %collective-permute-done = f32[1,512,128]{2,1,0:T(8,128)S(1)} collective-permute-done((f32[1,512,128]{2,1,0:T(8,128)S(1)}, f32[1,512,128]{2,1,0:T(8,128)S(1)}, u32[]{:S(2)}, u32[]{:S(2)}) %collective-permute-start) | collective-permute-done | bytes 262176 | tf_op jit(solution)/shard_map/ppermute | solution.py:205
  10.5 5.2 %collective-permute-done.2 = f32[1,512,128]{2,1,0:T(8,128)S(1)} collective-permute-done((f32[1,512,128]{2,1,0:T(8,128)S(1)}, f32[1,512,128]{2,1,0:T(8,128)S(1)}, u32[]{:S(2)}, u32[]{:S(2)}) %collective-permute-start.2) | collective-permute-done | bytes 262176 | tf_op jit(solution)/shard_map/ppermute | solution.py:205
  15.8 1.3 %collective-permute-start.7 = (f32[2,512,128]{2,1,0:T(8,128)S(1)}, f32[2,512,128]{2,1,0:T(8,128)S(1)}, u32[]{:S(2)}, u32[]{:S(2)}) collective-permute-start(f32[2,512,128]{2,1,0:T(8,128)S(1)} %constant_dynamic-update-slice_fusion.refs_0_.far), channel_id=1, source_target_pairs={{0,2},{1,5},{2,0},{8,10},{9,13},{10,8},{16,18},{17,21},{18,16},{24... | collective-permute-start | bytes 1572872 | tf_op jit(solution)/shard_map/ppermute | solution.py:185
  17.1 0.0 collective-permute-done.3.refs_1_
  17.1 2.5 %collective-permute-start.4 = (f32[2,512,128]{2,1,0:T(8,128)S(1)}, f32[2,512,128]{2,1,0:T(8,128)S(1)}, u32[]{:S(2)}, u32[]{:S(2)}) collective-permute-start(f32[2,512,128]{2,1,0:T(8,128)S(1)} %collective-permute-done.3.refs_1_), channel_id=1, source_target_pairs={{2,6},{5,7},{0,4},{10,14},{13,15},{8,12},{18,22},{21,23},{16,20},{... | collective-permute-start | bytes 1572872 | tf_op jit(solution)/shard_map/ppermute | solution.py:185
  19.6 8.5 %collective-permute-done.7.refs_1_ = f32[2,512,128]{2,1,0:T(8,128)S(1)} collective-permute-done((f32[2,512,128]{2,1,0:T(8,128)S(1)}, f32[2,512,128]{2,1,0:T(8,128)S(1)}, u32[]{:S(2)}, u32[]{:S(2)}) %collective-permute-start.7) | collective-permute-done | bytes 524320 | tf_op jit(solution)/shard_map/ppermute | solution.py:185
  28.1 1.3 %collective-permute-start.8 = (f32[2,512,128]{2,1,0:T(8,128)S(1)}, f32[2,512,128]{2,1,0:T(8,128)S(1)}, u32[]{:S(2)}, u32[]{:S(2)}) collective-permute-start(f32[2,512,128]{2,1,0:T(8,128)S(1)} %collective-permute-done.7.refs_1_), channel_id=1, source_target_pairs={{2,6},{5,7},{0,4},{10,14},{13,15},{8,12},{18,22},{21,23},{16,20},{... | collective-permute-start | bytes 1572872 | tf_op jit(solution)/shard_map/ppermute | solution.py:185
  29.4 1.3 %collective-permute-start.1 = (f32[1,512,128]{2,1,0:T(8,128)S(1)}, f32[1,512,128]{2,1,0:T(8,128)S(1)}, u32[]{:S(2)}, u32[]{:S(2)}) collective-permute-start(f32[1,512,128]{2,1,0:T(8,128)S(1)} %bitcast.8), channel_id=1, source_target_pairs={{0,16},{8,24},{16,0},{1,17},{9,25},{17,1},{2,18},{10,26},{18,2},{3... | collective-permute-start | bytes 786440 | tf_op jit(solution)/shard_map/ppermute | solution.py:205
  30.7 0.0 collective-permute-done.4.refs_2_
  30.7 0.7 collective-permute-start.5
  31.4 5.0 %collective-permute-done.8.refs_2_ = f32[2,512,128]{2,1,0:T(8,128)S(1)} collective-permute-done((f32[2,512,128]{2,1,0:T(8,128)S(1)}, f32[2,512,128]{2,1,0:T(8,128)S(1)}, u32[]{:S(2)}, u32[]{:S(2)}) %collective-permute-start.8) | collective-permute-done | bytes 524320 | tf_op jit(solution)/shard_map/ppermute | solution.py:185
  36.4 0.7 collective-permute-start.9
  37.1 0.5 collective-permute-done.1.refs_0_.near
  37.6 1.3 %collective-permute-start.11 = (f32[1,512,128]{2,1,0:T(8,128)S(1)}, f32[1,512,128]{2,1,0:T(8,128)S(1)}, u32[]{:S(2)}, u32[]{:S(2)}) collective-permute-start(f32[1,512,128]{2,1,0:T(8,128)S(1)} %collective-permute-done.1.refs_0_.near), channel_id=1, source_target_pairs={{0,2},{1,5},{2,0},{8,10},{9,13},{10,8},{16,18},{17,21},{18,16},{24... | collective-permute-start | bytes 786440 | tf_op jit(solution)/shard_map/ppermute | solution.py:185
  38.9 6.1 %collective-permute-done.11.refs_1_ = f32[1,512,128]{2,1,0:T(8,128)S(1)} collective-permute-done((f32[1,512,128]{2,1,0:T(8,128)S(1)}, f32[1,512,128]{2,1,0:T(8,128)S(1)}, u32[]{:S(2)}, u32[]{:S(2)}) %collective-permute-start.11) | collective-permute-done | bytes 262176 | tf_op jit(solution)/shard_map/ppermute | solution.py:185
  45.0 1.3 %collective-permute-start.12 = (f32[1,512,128]{2,1,0:T(8,128)S(1)}, f32[1,512,128]{2,1,0:T(8,128)S(1)}, u32[]{:S(2)}, u32[]{:S(2)}) collective-permute-start(f32[1,512,128]{2,1,0:T(8,128)S(1)} %collective-permute-done.11.refs_1_), channel_id=1, source_target_pairs={{2,6},{5,7},{0,4},{10,14},{13,15},{8,12},{18,22},{21,23},{16,20},{... | collective-permute-start | bytes 786440 | tf_op jit(solution)/shard_map/ppermute | solution.py:185
  46.3 0.0 collective-permute-done.5.refs_3_
  46.3 0.1 shard_map.17.own_mine
  46.4 0.1 collective-permute-start.6
  46.5 0.0 collective-permute-done.9.refs_3_
  46.5 0.1 shard_map.18.far_mine
  46.6 2.2 %collective-permute-start.10 = (f32[2,2,512,128]{3,2,1,0:T(8,128)S(1)}, f32[2,2,512,128]{3,2,1,0:T(8,128)S(1)}, u32[]{:S(2)}, u32[]{:S(2)}) collective-permute-start(f32[2,2,512,128]{3,2,1,0:T(8,128)S(1)} %shard_map.18.far_mine), channel_id=1, source_target_pairs={{0,1},{1,0},{2,3},{3,2},{4,5},{5,4},{6,7},{7,6},{8,9},{9,8},{10,11... | collective-permute-start | bytes 3145736 | tf_op jit(solution)/shard_map/ppermute | solution.py:191
  48.8 1.2 %collective-permute-done.12.refs_2_ = f32[1,512,128]{2,1,0:T(8,128)S(1)} collective-permute-done((f32[1,512,128]{2,1,0:T(8,128)S(1)}, f32[1,512,128]{2,1,0:T(8,128)S(1)}, u32[]{:S(2)}, u32[]{:S(2)}) %collective-permute-start.12) | collective-permute-done | bytes 262176 | tf_op jit(solution)/shard_map/ppermute | solution.py:185
  50.0 0.7 collective-permute-start.13
  50.7 0.0 collective-permute-done.13.refs_3_
  50.7 0.1 shard_map.19.near_mine
  50.7 14.1 %collective-permute-start.14 = (f32[2,1,512,128]{3,2,1,0:T(8,128)S(1)}, f32[2,1,512,128]{3,2,1,0:T(8,128)S(1)}, u32[]{:S(2)}, u32[]{:S(2)}) collective-permute-start(f32[2,1,512,128]{3,2,1,0:T(8,128)S(1)} %shard_map.19.near_mine), channel_id=1, source_target_pairs={{0,1},{1,0},{2,3},{3,2},{4,5},{5,4},{6,7},{7,6},{8,9},{9,8},{10,11... | collective-permute-start | bytes 1572872 | tf_op jit(solution)/shard_map/ppermute | solution.py:191
  64.9 1.5 %collective-permute-done.14.near_other = f32[2,1,512,128]{3,2,1,0:T(8,128)S(1)} collective-permute-done((f32[2,1,512,128]{3,2,1,0:T(8,128)S(1)}, f32[2,1,512,128]{3,2,1,0:T(8,128)S(1)}, u32[]{:S(2)}, u32[]{:S(2)}) %collective-permute-start.14) | collective-permute-done | bytes 524320 | tf_op jit(solution)/shard_map/ppermute | solution.py:191
  66.4 0.0 collective-permute-done.6.own_other
  66.4 0.0 collective-permute-done.10.far_other
  66.4 6.7 %shard_map.20 = f32[2,512,128]{2,1,0:T(8,128)} custom-call(f32[2,512,128]{2,1,0:T(8,128)S(1)} %bitcast.5, f32[1,512,128]{2,1,0:T(8,128)S(1)} %collective-permute-done.1.refs_0_.near, f32[2,512,128]{2,1,0:T(8,128)S(1)} %constant_dynamic-update-slice_fusion.refs_0_.far, f32[2,2,512,128]{3,2,1,0:T(8,128)S(1)} %shard_map.17.own_mine, ...), custom_call_target="tpu_custom_call" | custom-call | tf_op jit(solution)/shard_map/pallas_call | solution.py:133
  (2 shorter events, 0.0 us)
Async XLA Ops:
  0.0 3.8 %copy-start = (f32[2,1,256,1,256]{4,3,2,1,0:T(1,128)S(1)}, f32[2,1,256,1,256]{4,3,2,1,0:T(1,128)}, u32[]{:S(2)}) copy-start(f32[2,1,256,1,256]{4,3,2,1,0:T(1,128)} %param.1) | copy-start | bytes 1572868
  1.2 9.3 %collective-permute-start = (f32[1,512,128]{2,1,0:T(8,128)S(1)}, f32[1,512,128]{2,1,0:T(8,128)S(1)}, u32[]{:S(2)}, u32[]{:S(2)}) collective-permute-start(f32[1,512,128]{2,1,0:T(8,128)S(1)} %bitcast.6), channel_id=1, source_target_pairs={{0,8},{8,16},{16,24},{1,9},{9,17},{17,25},{2,10},{10,18},{18,26},{... | collective-permute-start | bytes 786440 | tf_op jit(solution)/shard_map/ppermute | solution.py:205
  2.5 13.2 %collective-permute-start.2 = (f32[1,512,128]{2,1,0:T(8,128)S(1)}, f32[1,512,128]{2,1,0:T(8,128)S(1)}, u32[]{:S(2)}, u32[]{:S(2)}) collective-permute-start(f32[1,512,128]{2,1,0:T(8,128)S(1)} %bitcast.7), channel_id=1, source_target_pairs={{0,24},{8,0},{16,8},{1,25},{9,1},{17,9},{2,26},{10,2},{18,10},{3,2... | collective-permute-start | bytes 786440 | tf_op jit(solution)/shard_map/ppermute | solution.py:205
  3.8 13.2 %collective-permute-start.3 = (f32[2,512,128]{2,1,0:T(8,128)S(1)}, f32[2,512,128]{2,1,0:T(8,128)S(1)}, u32[]{:S(2)}, u32[]{:S(2)}) collective-permute-start(f32[2,512,128]{2,1,0:T(8,128)S(1)} %bitcast.3), channel_id=1, source_target_pairs={{0,2},{1,5},{2,0},{8,10},{9,13},{10,8},{16,18},{17,21},{18,16},{24... | collective-permute-start | bytes 1572872 | tf_op jit(solution)/shard_map/ppermute | solution.py:185
  15.8 12.3 %collective-permute-start.7 = (f32[2,512,128]{2,1,0:T(8,128)S(1)}, f32[2,512,128]{2,1,0:T(8,128)S(1)}, u32[]{:S(2)}, u32[]{:S(2)}) collective-permute-start(f32[2,512,128]{2,1,0:T(8,128)S(1)} %constant_dynamic-update-slice_fusion.refs_0_.far), channel_id=1, source_target_pairs={{0,2},{1,5},{2,0},{8,10},{9,13},{10,8},{16,18},{17,21},{18,16},{24... | collective-permute-start | bytes 1572872 | tf_op jit(solution)/shard_map/ppermute | solution.py:185
  17.1 13.7 %collective-permute-start.4 = (f32[2,512,128]{2,1,0:T(8,128)S(1)}, f32[2,512,128]{2,1,0:T(8,128)S(1)}, u32[]{:S(2)}, u32[]{:S(2)}) collective-permute-start(f32[2,512,128]{2,1,0:T(8,128)S(1)} %collective-permute-done.3.refs_1_), channel_id=1, source_target_pairs={{2,6},{5,7},{0,4},{10,14},{13,15},{8,12},{18,22},{21,23},{16,20},{... | collective-permute-start | bytes 1572872 | tf_op jit(solution)/shard_map/ppermute | solution.py:185
  28.1 8.3 %collective-permute-start.8 = (f32[2,512,128]{2,1,0:T(8,128)S(1)}, f32[2,512,128]{2,1,0:T(8,128)S(1)}, u32[]{:S(2)}, u32[]{:S(2)}) collective-permute-start(f32[2,512,128]{2,1,0:T(8,128)S(1)} %collective-permute-done.7.refs_1_), channel_id=1, source_target_pairs={{2,6},{5,7},{0,4},{10,14},{13,15},{8,12},{18,22},{21,23},{16,20},{... | collective-permute-start | bytes 1572872 | tf_op jit(solution)/shard_map/ppermute | solution.py:185
  29.4 8.2 %collective-permute-start.1 = (f32[1,512,128]{2,1,0:T(8,128)S(1)}, f32[1,512,128]{2,1,0:T(8,128)S(1)}, u32[]{:S(2)}, u32[]{:S(2)}) collective-permute-start(f32[1,512,128]{2,1,0:T(8,128)S(1)} %bitcast.8), channel_id=1, source_target_pairs={{0,16},{8,24},{16,0},{1,17},{9,25},{17,1},{2,18},{10,26},{18,2},{3... | collective-permute-start | bytes 786440 | tf_op jit(solution)/shard_map/ppermute | solution.py:205
  30.7 15.6 %collective-permute-start.5 = (f32[2,512,128]{2,1,0:T(8,128)S(1)}, f32[2,512,128]{2,1,0:T(8,128)S(1)}, u32[]{:S(2)}, u32[]{:S(2)}) collective-permute-start(f32[2,512,128]{2,1,0:T(8,128)S(1)} %collective-permute-done.4.refs_2_), channel_id=1, source_target_pairs={{6,4},{7,3},{4,6},{14,12},{15,11},{12,14},{22,20},{23,19},{20,22},... | collective-permute-start | bytes 1572872 | tf_op jit(solution)/shard_map/ppermute | solution.py:185
  36.4 10.1 %collective-permute-start.9 = (f32[2,512,128]{2,1,0:T(8,128)S(1)}, f32[2,512,128]{2,1,0:T(8,128)S(1)}, u32[]{:S(2)}, u32[]{:S(2)}) collective-permute-start(f32[2,512,128]{2,1,0:T(8,128)S(1)} %collective-permute-done.8.refs_2_), channel_id=1, source_target_pairs={{6,4},{7,3},{4,6},{14,12},{15,11},{12,14},{22,20},{23,19},{20,22},... | collective-permute-start | bytes 1572872 | tf_op jit(solution)/shard_map/ppermute | solution.py:185
  37.6 7.4 %collective-permute-start.11 = (f32[1,512,128]{2,1,0:T(8,128)S(1)}, f32[1,512,128]{2,1,0:T(8,128)S(1)}, u32[]{:S(2)}, u32[]{:S(2)}) collective-permute-start(f32[1,512,128]{2,1,0:T(8,128)S(1)} %collective-permute-done.1.refs_0_.near), channel_id=1, source_target_pairs={{0,2},{1,5},{2,0},{8,10},{9,13},{10,8},{16,18},{17,21},{18,16},{24... | collective-permute-start | bytes 786440 | tf_op jit(solution)/shard_map/ppermute | solution.py:185
  45.0 5.0 %collective-permute-start.12 = (f32[1,512,128]{2,1,0:T(8,128)S(1)}, f32[1,512,128]{2,1,0:T(8,128)S(1)}, u32[]{:S(2)}, u32[]{:S(2)}) collective-permute-start(f32[1,512,128]{2,1,0:T(8,128)S(1)} %collective-permute-done.11.refs_1_), channel_id=1, source_target_pairs={{2,6},{5,7},{0,4},{10,14},{13,15},{8,12},{18,22},{21,23},{16,20},{... | collective-permute-start | bytes 786440 | tf_op jit(solution)/shard_map/ppermute | solution.py:185
  46.4 20.0 %collective-permute-start.6 = (f32[2,2,512,128]{3,2,1,0:T(8,128)S(1)}, f32[2,2,512,128]{3,2,1,0:T(8,128)S(1)}, u32[]{:S(2)}, u32[]{:S(2)}) collective-permute-start(f32[2,2,512,128]{3,2,1,0:T(8,128)S(1)} %shard_map.17.own_mine), channel_id=1, source_target_pairs={{0,1},{1,0},{2,3},{3,2},{4,5},{5,4},{6,7},{7,6},{8,9},{9,8},{10,11... | collective-permute-start | bytes 3145736 | tf_op jit(solution)/shard_map/ppermute | solution.py:191
  46.6 19.9 %collective-permute-start.10 = (f32[2,2,512,128]{3,2,1,0:T(8,128)S(1)}, f32[2,2,512,128]{3,2,1,0:T(8,128)S(1)}, u32[]{:S(2)}, u32[]{:S(2)}) collective-permute-start(f32[2,2,512,128]{3,2,1,0:T(8,128)S(1)} %shard_map.18.far_mine), channel_id=1, source_target_pairs={{0,1},{1,0},{2,3},{3,2},{4,5},{5,4},{6,7},{7,6},{8,9},{9,8},{10,11... | collective-permute-start | bytes 3145736 | tf_op jit(solution)/shard_map/ppermute | solution.py:191
  50.0 0.7 collective-permute-start.13
  50.7 15.7 %collective-permute-start.14 = (f32[2,1,512,128]{3,2,1,0:T(8,128)S(1)}, f32[2,1,512,128]{3,2,1,0:T(8,128)S(1)}, u32[]{:S(2)}, u32[]{:S(2)}) collective-permute-start(f32[2,1,512,128]{3,2,1,0:T(8,128)S(1)} %shard_map.19.near_mine), channel_id=1, source_target_pairs={{0,1},{1,0},{2,3},{3,2},{4,5},{5,4},{6,7},{7,6},{8,9},{9,8},{10,11... | collective-permute-start | bytes 1572872 | tf_op jit(solution)/shard_map/ppermute | solution.py:191

commit v2 on v0

--- a/solution.py
+++ b/solution.py
@@ -157,11 +157,25 @@
                 mine[slot] = source[...]
 
 
+def relay_kernel(even_ref, odd_ref, out):
+    even = lax.rem(lax.axis_index("pcol"), 2) == 0
+
+    @pl.when(even)
+    def _():
+        out[...] = even_ref[...]
+
+    @pl.when(jnp.logical_not(even))
+    def _():
+        out[...] = odd_ref[...]
+
+
 def arrivals(block):
     arrived = {0: block}
     for mask in range(2, lax.axis_size("pcol"), 2):
-        before = mask & (mask - 1)
-        arrived[mask] = lax.ppermute(arrived[before], "pcol", [(c ^ before, c ^ mask) for c in range(PANELS)])
+        before = (mask & (mask - 1), mask ^ (1 << (mask.bit_length() - 1)))
+        even, odd = arrived[before[0]], arrived[before[1]]
+        payload = even if before[0] == before[1] else in_vmem(relay_kernel, block.shape, [even, odd])
+        arrived[mask] = lax.ppermute(payload, "pcol", [(c ^ before[c % 2], c ^ mask) for c in range(PANELS)])
     return [arrived[mask] for mask in sorted(arrived)]
 
 

time: 73.1 us -> 74.6 us (1.021)
  starting transfers between devices: 25.1 us -> 34 us
  waiting for transfers between devices: 39.3 us -> 31.9 us
    ppermute x3, starting transfers between devices: 10.9 us -> 22.1 us  [exchange(): lax.ppermute(mine, 'pcol', [(c, c ^ 1) for c in range(lax.axis_size('pcol...]
    ppermute x3, waiting for transfers between devices: 23.5 us -> 19.4 us  [from_rows(): lax.ppermute(block, 'prow', [(k, (k + d) % row_count) for k in range(PANE...]
    ppermute x9, waiting for transfers between devices: 14.2 us -> 10.9 us  [arrivals(): lax.ppermute(payload, 'pcol', [(c ^ before[c % 2], c ^ mask) for c in ran...]
    ppermute x9, starting transfers between devices: 10.3 us -> 8 us  [arrivals(): lax.ppermute(payload, 'pcol', [(c ^ before[c % 2], c ^ mask) for c in ran...]
    pallas_call x4 -> x7, Pallas kernels: 6.93 us -> 7.04 us  [in_vmem(): pl.pallas_call(kernel, out_shape=jax.ShapeDtypeStruct(out_shape, jnp.floa...]
  transfers between devices with their start and end apart: 15 -> 15, of which waited for: 8 -> 6; matrix products, arithmetic and copies ran while one was open for 0% -> 0% of each run, Pallas kernels for 0% -> 0%
where the time goes in v2:
time: 74.6 us; the launch traced here: 74.3 us
  starting transfers between devices  34 us (46%)
  waiting for transfers between devices  31.9 us (43%)
  Pallas kernels  7.04 us (9%)
  local copies, waits for them, and re-layouts  1.24 us (2%)
    ppermute x3, starting transfers between devices, exchange(): lax.ppermute(mine, 'pcol', [(c, c ^ 1) for c in range(lax.axis_size('pcol...  22.1 us
    ppermute x3, waiting for transfers between devices, from_rows(): lax.ppermute(block, 'prow', [(k, (k + d) % row_count) for k in range(PANE...  19.4 us
    ppermute x9, waiting for transfers between devices, arrivals(): lax.ppermute(payload, 'pcol', [(c ^ before[c % 2], c ^ mask) for c in ran...  10.9 us
    ppermute x9, starting transfers between devices, arrivals(): lax.ppermute(payload, 'pcol', [(c ^ before[c % 2], c ^ mask) for c in ran...  8 us
    pallas_call x7, Pallas kernels, in_vmem(): pl.pallas_call(kernel, out_shape=jax.ShapeDtypeStruct(out_shape, jnp.floa...  7.04 us
    ppermute x3, starting transfers between devices, from_rows(): lax.ppermute(block, 'prow', [(k, (k + d) % row_count) for k in range(PANE...  3.88 us
    ppermute x3, waiting for transfers between devices, exchange(): lax.ppermute(mine, 'pcol', [(c, c ^ 1) for c in range(lax.axis_size('pcol...  1.54 us
  transfers between devices with their start and end apart: 15, of which 6 were waited for; matrix products, arithmetic and copies ran while one was open for 0% of the time, Pallas kernels for 0%

profile of v2, /device:TPU:29, one launch (start us, length us, event | category | flops | bytes accessed | tf_op | source)
XLA Modules:
  0.0 74.3 jit_solution(4479599023164127438)
XLA Ops:
  0.0 0.0 copy-start
  0.0 1.2 %slice.8 = f32[1,1,256,1,256]{4,3,2,1,0:T(1,128)S(1)} slice(f32[2,1,256,1,256]{4,3,2,1,0:T(1,128)} %param.1), slice={[0:1], [0:1], [0:256], [0:1], [0:256]} | slice | bytes 524288 | tf_op jit(solution)/shard_map/slice | solution.py:204
  1.2 1.3 %collective-permute-start = (f32[1,512,128]{2,1,0:T(8,128)S(1)}, f32[1,512,128]{2,1,0:T(8,128)S(1)}, u32[]{:S(2)}, u32[]{:S(2)}) collective-permute-start(f32[1,512,128]{2,1,0:T(8,128)S(1)} %bitcast.7), channel_id=1, source_target_pairs={{0,8},{8,16},{16,24},{1,9},{9,17},{17,25},{2,10},{10,18},{18,26},{... | collective-permute-start | bytes 786440 | tf_op jit(solution)/shard_map/ppermute | solution.py:198
  2.5 1.3 %collective-permute-start.2 = (f32[1,512,128]{2,1,0:T(8,128)S(1)}, f32[1,512,128]{2,1,0:T(8,128)S(1)}, u32[]{:S(2)}, u32[]{:S(2)}) collective-permute-start(f32[1,512,128]{2,1,0:T(8,128)S(1)} %bitcast.8), channel_id=1, source_target_pairs={{0,24},{8,0},{16,8},{1,25},{9,1},{17,9},{2,26},{10,2},{18,10},{3,2... | collective-permute-start | bytes 786440 | tf_op jit(solution)/shard_map/ppermute | solution.py:198
  3.8 0.0 copy-done
  3.8 1.3 %collective-permute-start.4 = (f32[2,512,128]{2,1,0:T(8,128)S(1)}, f32[2,512,128]{2,1,0:T(8,128)S(1)}, u32[]{:S(2)}, u32[]{:S(2)}) collective-permute-start(f32[2,512,128]{2,1,0:T(8,128)S(1)} %bitcast.3), channel_id=1, source_target_pairs={{0,4},{1,5},{2,6},{8,12},{9,13},{10,14},{16,20},{17,21},{18,22},{2... | collective-permute-start | bytes 1572872 | tf_op jit(solution)/shard_map/ppermute | solution.py:178
  5.1 0.7 collective-permute-start.3
  5.8 4.7 %collective-permute-done = f32[1,512,128]{2,1,0:T(8,128)S(1)} collective-permute-done((f32[1,512,128]{2,1,0:T(8,128)S(1)}, f32[1,512,128]{2,1,0:T(8,128)S(1)}, u32[]{:S(2)}, u32[]{:S(2)}) %collective-permute-start) | collective-permute-done | bytes 262176 | tf_op jit(solution)/shard_map/ppermute | solution.py:198
  10.5 5.2 %collective-permute-done.2 = f32[1,512,128]{2,1,0:T(8,128)S(1)} collective-permute-done((f32[1,512,128]{2,1,0:T(8,128)S(1)}, f32[1,512,128]{2,1,0:T(8,128)S(1)}, u32[]{:S(2)}, u32[]{:S(2)}) %collective-permute-start.2) | collective-permute-done | bytes 262176 | tf_op jit(solution)/shard_map/ppermute | solution.py:198
  15.8 1.3 %collective-permute-start.8 = (f32[2,512,128]{2,1,0:T(8,128)S(1)}, f32[2,512,128]{2,1,0:T(8,128)S(1)}, u32[]{:S(2)}, u32[]{:S(2)}) collective-permute-start(f32[2,512,128]{2,1,0:T(8,128)S(1)} %constant_dynamic-update-slice_fusion.refs_0_.far), channel_id=1, source_target_pairs={{0,4},{1,5},{2,6},{8,12},{9,13},{10,14},{16,20},{17,21},{18,22},{2... | collective-permute-start | bytes 1572872 | tf_op jit(solution)/shard_map/ppermute | solution.py:178
  17.1 0.7 collective-permute-start.7
  17.8 0.8 %collective-permute-done.4.even_ref.refs_2_ = f32[2,512,128]{2,1,0:T(8,128)S(1)} collective-permute-done((f32[2,512,128]{2,1,0:T(8,128)S(1)}, f32[2,512,128]{2,1,0:T(8,128)S(1)}, u32[]{:S(2)}, u32[]{:S(2)}) %collective-permute-start.4) | collective-permute-done | bytes 524320 | tf_op jit(solution)/shard_map/ppermute | solution.py:178
  18.5 0.0 collective-permute-done.3.odd_ref.refs_1_
  18.6 0.7 collective-permute-start.5
  19.3 10.1 %collective-permute-done.8.even_ref.refs_2_ = f32[2,512,128]{2,1,0:T(8,128)S(1)} collective-permute-done((f32[2,512,128]{2,1,0:T(8,128)S(1)}, f32[2,512,128]{2,1,0:T(8,128)S(1)}, u32[]{:S(2)}, u32[]{:S(2)}) %collective-permute-start.8) | collective-permute-done | bytes 524320 | tf_op jit(solution)/shard_map/ppermute | solution.py:178
  29.4 0.0 collective-permute-done.7.odd_ref.refs_1_
  29.4 0.7 collective-permute-start.9
  30.1 1.3 %collective-permute-start.1 = (f32[1,512,128]{2,1,0:T(8,128)S(1)}, f32[1,512,128]{2,1,0:T(8,128)S(1)}, u32[]{:S(2)}, u32[]{:S(2)}) collective-permute-start(f32[1,512,128]{2,1,0:T(8,128)S(1)} %bitcast.9), channel_id=1, source_target_pairs={{0,16},{8,24},{16,0},{1,17},{9,25},{17,1},{2,18},{10,26},{18,2},{3... | collective-permute-start | bytes 786440 | tf_op jit(solution)/shard_map/ppermute | solution.py:198
  31.4 9.5 %collective-permute-done.1.refs_0_.near = f32[1,512,128]{2,1,0:T(8,128)S(1)} collective-permute-done((f32[1,512,128]{2,1,0:T(8,128)S(1)}, f32[1,512,128]{2,1,0:T(8,128)S(1)}, u32[]{:S(2)}, u32[]{:S(2)}) %collective-permute-start.1) | collective-permute-done | bytes 262176 | tf_op jit(solution)/shard_map/ppermute | solution.py:198
  40.9 1.3 %collective-permute-start.12 = (f32[1,512,128]{2,1,0:T(8,128)S(1)}, f32[1,512,128]{2,1,0:T(8,128)S(1)}, u32[]{:S(2)}, u32[]{:S(2)}) collective-permute-start(f32[1,512,128]{2,1,0:T(8,128)S(1)} %collective-permute-done.1.refs_0_.near), channel_id=1, source_target_pairs={{0,4},{1,5},{2,6},{8,12},{9,13},{10,14},{16,20},{17,21},{18,22},{2... | collective-permute-start | bytes 786440 | tf_op jit(solution)/shard_map/ppermute | solution.py:178
  42.2 0.7 collective-permute-start.11
  42.9 0.0 collective-permute-done.5.refs_3_
  42.9 0.1 shard_map.18.own_mine
  43.0 8.5 %collective-permute-start.6 = (f32[2,2,512,128]{3,2,1,0:T(8,128)S(1)}, f32[2,2,512,128]{3,2,1,0:T(8,128)S(1)}, u32[]{:S(2)}, u32[]{:S(2)}) collective-permute-start(f32[2,2,512,128]{3,2,1,0:T(8,128)S(1)} %shard_map.18.own_mine), channel_id=1, source_target_pairs={{0,1},{1,0},{2,3},{3,2},{4,5},{5,4},{6,7},{7,6},{8,9},{9,8},{10,11... | collective-permute-start | bytes 3145736 | tf_op jit(solution)/shard_map/ppermute | solution.py:184
  51.5 0.0 collective-permute-done.9.refs_3_
  51.5 0.1 shard_map.20.far_mine
  51.6 0.1 collective-permute-start.10
  51.7 0.0 collective-permute-done.12.even_ref.refs_2_
  51.7 0.0 collective-permute-done.11.odd_ref.refs_1_
  51.8 0.7 collective-permute-start.13
  52.4 0.0 collective-permute-done.13.refs_3_
  52.4 0.1 shard_map.22.near_mine
  52.5 13.5 %collective-permute-start.14 = (f32[2,1,512,128]{3,2,1,0:T(8,128)S(1)}, f32[2,1,512,128]{3,2,1,0:T(8,128)S(1)}, u32[]{:S(2)}, u32[]{:S(2)}) collective-permute-start(f32[2,1,512,128]{3,2,1,0:T(8,128)S(1)} %shard_map.22.near_mine), channel_id=1, source_target_pairs={{0,1},{1,0},{2,3},{3,2},{4,5},{5,4},{6,7},{7,6},{8,9},{9,8},{10,11... | collective-permute-start | bytes 1572872 | tf_op jit(solution)/shard_map/ppermute | solution.py:184
  66.0 1.5 %collective-permute-done.14.near_other = f32[2,1,512,128]{3,2,1,0:T(8,128)S(1)} collective-permute-done((f32[2,1,512,128]{3,2,1,0:T(8,128)S(1)}, f32[2,1,512,128]{3,2,1,0:T(8,128)S(1)}, u32[]{:S(2)}, u32[]{:S(2)}) %collective-permute-start.14) | collective-permute-done | bytes 524320 | tf_op jit(solution)/shard_map/ppermute | solution.py:184
  67.6 0.0 collective-permute-done.6.own_other
  67.6 0.0 collective-permute-done.10.far_other
  67.6 6.7 %shard_map.23 = f32[2,512,128]{2,1,0:T(8,128)} custom-call(f32[2,512,128]{2,1,0:T(8,128)S(1)} %bitcast.6, f32[1,512,128]{2,1,0:T(8,128)S(1)} %collective-permute-done.1.refs_0_.near, f32[2,512,128]{2,1,0:T(8,128)S(1)} %constant_dynamic-update-slice_fusion.refs_0_.far, f32[2,2,512,128]{3,2,1,0:T(8,128)S(1)} %shard_map.18.own_mine, ...), custom_call_target="tpu_custom_call" | custom-call | tf_op jit(solution)/shard_map/pallas_call | solution.py:133
  (5 shorter events, 0.1 us)
Async XLA Ops:
  0.0 3.8 %copy-start = (f32[2,1,256,1,256]{4,3,2,1,0:T(1,128)S(1)}, f32[2,1,256,1,256]{4,3,2,1,0:T(1,128)}, u32[]{:S(2)}) copy-start(f32[2,1,256,1,256]{4,3,2,1,0:T(1,128)} %param.1) | copy-start | bytes 1572868
  1.2 9.3 %collective-permute-start = (f32[1,512,128]{2,1,0:T(8,128)S(1)}, f32[1,512,128]{2,1,0:T(8,128)S(1)}, u32[]{:S(2)}, u32[]{:S(2)}) collective-permute-start(f32[1,512,128]{2,1,0:T(8,128)S(1)} %bitcast.7), channel_id=1, source_target_pairs={{0,8},{8,16},{16,24},{1,9},{9,17},{17,25},{2,10},{10,18},{18,26},{... | collective-permute-start | bytes 786440 | tf_op jit(solution)/shard_map/ppermute | solution.py:198
  2.5 13.2 %collective-permute-start.2 = (f32[1,512,128]{2,1,0:T(8,128)S(1)}, f32[1,512,128]{2,1,0:T(8,128)S(1)}, u32[]{:S(2)}, u32[]{:S(2)}) collective-permute-start(f32[1,512,128]{2,1,0:T(8,128)S(1)} %bitcast.8), channel_id=1, source_target_pairs={{0,24},{8,0},{16,8},{1,25},{9,1},{17,9},{2,26},{10,2},{18,10},{3,2... | collective-permute-start | bytes 786440 | tf_op jit(solution)/shard_map/ppermute | solution.py:198
  3.8 14.7 %collective-permute-start.4 = (f32[2,512,128]{2,1,0:T(8,128)S(1)}, f32[2,512,128]{2,1,0:T(8,128)S(1)}, u32[]{:S(2)}, u32[]{:S(2)}) collective-permute-start(f32[2,512,128]{2,1,0:T(8,128)S(1)} %bitcast.3), channel_id=1, source_target_pairs={{0,4},{1,5},{2,6},{8,12},{9,13},{10,14},{16,20},{17,21},{18,22},{2... | collective-permute-start | bytes 1572872 | tf_op jit(solution)/shard_map/ppermute | solution.py:178
  5.1 13.4 %collective-permute-start.3 = (f32[2,512,128]{2,1,0:T(8,128)S(1)}, f32[2,512,128]{2,1,0:T(8,128)S(1)}, u32[]{:S(2)}, u32[]{:S(2)}) collective-permute-start(f32[2,512,128]{2,1,0:T(8,128)S(1)} %bitcast.4), channel_id=1, source_target_pairs={{0,2},{1,3},{2,0},{8,10},{9,11},{10,8},{16,18},{17,19},{18,16},{24... | collective-permute-start | bytes 1572872 | tf_op jit(solution)/shard_map/ppermute | solution.py:178
  15.8 13.6 %collective-permute-start.8 = (f32[2,512,128]{2,1,0:T(8,128)S(1)}, f32[2,512,128]{2,1,0:T(8,128)S(1)}, u32[]{:S(2)}, u32[]{:S(2)}) collective-permute-start(f32[2,512,128]{2,1,0:T(8,128)S(1)} %constant_dynamic-update-slice_fusion.refs_0_.far), channel_id=1, source_target_pairs={{0,4},{1,5},{2,6},{8,12},{9,13},{10,14},{16,20},{17,21},{18,22},{2... | collective-permute-start | bytes 1572872 | tf_op jit(solution)/shard_map/ppermute | solution.py:178
  17.1 12.3 %collective-permute-start.7 = (f32[2,512,128]{2,1,0:T(8,128)S(1)}, f32[2,512,128]{2,1,0:T(8,128)S(1)}, u32[]{:S(2)}, u32[]{:S(2)}) collective-permute-start(f32[2,512,128]{2,1,0:T(8,128)S(1)} %constant_dynamic-update-slice_fusion.refs_0_.far), channel_id=1, source_target_pairs={{0,2},{1,3},{2,0},{8,10},{9,11},{10,8},{16,18},{17,19},{18,16},{24... | collective-permute-start | bytes 1572872 | tf_op jit(solution)/shard_map/ppermute | solution.py:178
  18.6 24.4 %collective-permute-start.5 = (f32[2,512,128]{2,1,0:T(8,128)S(1)}, f32[2,512,128]{2,1,0:T(8,128)S(1)}, u32[]{:S(2)}, u32[]{:S(2)}) collective-permute-start(f32[2,512,128]{2,1,0:T(8,128)S(1)} %shard_map.17), channel_id=1, source_target_pairs={{4,6},{3,7},{6,4},{12,14},{11,15},{14,12},{20,22},{19,23},{22,20},... | collective-permute-start | bytes 1572872 | tf_op jit(solution)/shard_map/ppermute | solution.py:178
  29.4 22.1 %collective-permute-start.9 = (f32[2,512,128]{2,1,0:T(8,128)S(1)}, f32[2,512,128]{2,1,0:T(8,128)S(1)}, u32[]{:S(2)}, u32[]{:S(2)}) collective-permute-start(f32[2,512,128]{2,1,0:T(8,128)S(1)} %shard_map.19), channel_id=1, source_target_pairs={{4,6},{3,7},{6,4},{12,14},{11,15},{14,12},{20,22},{19,23},{22,20},... | collective-permute-start | bytes 1572872 | tf_op jit(solution)/shard_map/ppermute | solution.py:178
  30.1 10.8 %collective-permute-start.1 = (f32[1,512,128]{2,1,0:T(8,128)S(1)}, f32[1,512,128]{2,1,0:T(8,128)S(1)}, u32[]{:S(2)}, u32[]{:S(2)}) collective-permute-start(f32[1,512,128]{2,1,0:T(8,128)S(1)} %bitcast.9), channel_id=1, source_target_pairs={{0,16},{8,24},{16,0},{1,17},{9,25},{17,1},{2,18},{10,26},{18,2},{3... | collective-permute-start | bytes 786440 | tf_op jit(solution)/shard_map/ppermute | solution.py:198
  40.9 10.8 %collective-permute-start.12 = (f32[1,512,128]{2,1,0:T(8,128)S(1)}, f32[1,512,128]{2,1,0:T(8,128)S(1)}, u32[]{:S(2)}, u32[]{:S(2)}) collective-permute-start(f32[1,512,128]{2,1,0:T(8,128)S(1)} %collective-permute-done.1.refs_0_.near), channel_id=1, source_target_pairs={{0,4},{1,5},{2,6},{8,12},{9,13},{10,14},{16,20},{17,21},{18,22},{2... | collective-permute-start | bytes 786440 | tf_op jit(solution)/shard_map/ppermute | solution.py:178
  42.2 9.5 %collective-permute-start.11 = (f32[1,512,128]{2,1,0:T(8,128)S(1)}, f32[1,512,128]{2,1,0:T(8,128)S(1)}, u32[]{:S(2)}, u32[]{:S(2)}) collective-permute-start(f32[1,512,128]{2,1,0:T(8,128)S(1)} %collective-permute-done.1.refs_0_.near), channel_id=1, source_target_pairs={{0,2},{1,3},{2,0},{8,10},{9,11},{10,8},{16,18},{17,19},{18,16},{24... | collective-permute-start | bytes 786440 | tf_op jit(solution)/shard_map/ppermute | solution.py:178
  43.0 24.5 %collective-permute-start.6 = (f32[2,2,512,128]{3,2,1,0:T(8,128)S(1)}, f32[2,2,512,128]{3,2,1,0:T(8,128)S(1)}, u32[]{:S(2)}, u32[]{:S(2)}) collective-permute-start(f32[2,2,512,128]{3,2,1,0:T(8,128)S(1)} %shard_map.18.own_mine), channel_id=1, source_target_pairs={{0,1},{1,0},{2,3},{3,2},{4,5},{5,4},{6,7},{7,6},{8,9},{9,8},{10,11... | collective-permute-start | bytes 3145736 | tf_op jit(solution)/shard_map/ppermute | solution.py:184
  51.6 16.0 %collective-permute-start.10 = (f32[2,2,512,128]{3,2,1,0:T(8,128)S(1)}, f32[2,2,512,128]{3,2,1,0:T(8,128)S(1)}, u32[]{:S(2)}, u32[]{:S(2)}) collective-permute-start(f32[2,2,512,128]{3,2,1,0:T(8,128)S(1)} %shard_map.20.far_mine), channel_id=1, source_target_pairs={{0,1},{1,0},{2,3},{3,2},{4,5},{5,4},{6,7},{7,6},{8,9},{9,8},{10,11... | collective-permute-start | bytes 3145736 | tf_op jit(solution)/shard_map/ppermute | solution.py:184
  51.8 0.7 collective-permute-start.13
  52.5 15.0 %collective-permute-start.14 = (f32[2,1,512,128]{3,2,1,0:T(8,128)S(1)}, f32[2,1,512,128]{3,2,1,0:T(8,128)S(1)}, u32[]{:S(2)}, u32[]{:S(2)}) collective-permute-start(f32[2,1,512,128]{3,2,1,0:T(8,128)S(1)} %shard_map.22.near_mine), channel_id=1, source_target_pairs={{0,1},{1,0},{2,3},{3,2},{4,5},{5,4},{6,7},{7,6},{8,9},{9,8},{10,11... | collective-permute-start | bytes 1572872 | tf_op jit(solution)/shard_map/ppermute | solution.py:184

commit v3 on v0

v3 whole, which is shorter than its diff:
```python
import functools
import math

import jax
import jax.numpy as jnp
from jax import lax
from jax.experimental import pallas as pl
from jax.experimental.pallas import tpu as pltpu
from jax.sharding import PartitionSpec as P


PANELS = 3


def split(value):
    high = value.astype(jnp.bfloat16)
    low = (value - high.astype(jnp.float32)).astype(jnp.bfloat16)
    return high, low


def product(left, right):
    dot = functools.partial(jnp.dot, preferred_element_type=jnp.float32)
    return dot(left[0], right[0]) + (dot(left[0], right[1]) + dot(left[1], right[0]))


def invert(block):
    size = block.shape[0]
    eye = lax.broadcasted_iota(jnp.int32, (size, size), 0) == lax.broadcasted_iota(jnp.int32, (size, size), 1)
    diagonal = jnp.where(eye, block, 0.0)
    down = 1.0 / jnp.sum(diagonal, axis=1, keepdims=True)
    along = 1.0 / jnp.sum(diagonal, axis=0, keepdims=True)
    first = jnp.where(eye, 2.0 * down, 0.0) - down * block * along
    parts = split(first)
    inner = product(split(block), parts)
    return 2.0 * first - product(parts, split(inner))


def distance_groups(row_count):
    groups = []
    for distance in range(1, row_count):
        targets = {(k + distance) % row_count for k in range(PANELS)}
        for group in groups:
            if not targets & group[1]:
                group[0].append(distance)
                group[1].update(targets)
                break
        else:
            groups.append(([distance], targets))
    groups = [group[0] for group in groups]
    return groups[:1] + groups[2:], groups[1]


LANES = 128


def load(ref, index, size):
    step = size // LANES
    return jnp.concatenate([ref[(*index, pl.ds(part, size, stride=step), slice(None))] for part in range(step)], axis=1)


def store(ref, index, value):
    size = value.shape[0]
    step = size // LANES
    for part in range(step):
        ref[(*index, pl.ds(part, size, stride=step), slice(None))] = value[:, part * LANES : (part + 1) * LANES]


def plane_kinds(row_count):
    kinds = {}
    for plane in range(row_count):
        late = [k for k in range(PANELS) if (plane - k) % row_count in distance_groups(row_count)[1]]
        kinds.setdefault((late[0] if late else None, plane < PANELS), []).append(plane)
    return kinds


def column(index, size):
    return slice(index * size, (index + 1) * size)


def place(work, target, mine, other, piece, own, own_index):
    size = work.shape[1]
    even = lax.rem(lax.axis_index("pcol"), 2) == 0
    work[target, :, column(PANELS, size)] = load(own, (own_index,), size)

    @pl.when(even)
    def _():
        work[target, :, column(0, size)] = load(mine, (0, piece), size)
        work[target, :, column(1, size)] = load(other, (0, piece), size)
        work[target, :, column(2, size)] = load(mine, (1, piece), size)

    @pl.when(jnp.logical_not(even))
    def _():
        work[target, :, column(0, size)] = load(other, (0, piece), size)
        work[target, :, column(1, size)] = load(mine, (0, piece), size)
        work[target, :, column(2, size)] = load(other, (1, piece), size)


def place_arrived(work, group, mine, other, piece, own):
    my_row, row_count = lax.axis_index("prow"), lax.axis_size("prow")
    for distance in group:
        source = lax.rem(my_row + row_count - distance, row_count)

        @pl.when(source < PANELS)
        def _():
            place(work, source, mine, other, piece, own, piece)


def run_panel(work, panel, rows, begin=True):
    size = work.shape[1]
    if begin:
        inverse = invert(work[panel, :, column(panel, size)])
        work[panel, :, column(panel, size)] = inverse
    else:
        inverse = work[panel, :, column(panel, size)]
    inverse = split(inverse)
    rest = slice((panel + 1) * size, (PANELS + 1) * size)
    pivot_row = split(work[panel, :, rest])
    for index in rows:
        factor = product(split(work[index, :, column(panel, size)]), inverse)
        work[index, :, column(panel, size)] = factor
        work[index, :, rest] = work[index, :, rest] - product(split(factor), pivot_row)


def for_kinds(count, run):
    my_row = lax.axis_index("prow")
    for (late, own_pivot), planes in plane_kinds(lax.axis_size("prow")).items():
        here = functools.reduce(jnp.logical_or, [my_row == plane for plane in planes])
        own = range(PANELS + (1 if own_pivot else 0), PANELS + count)

        @pl.when(here)
        def _():
            run(late, list(own))


def early_kernel(tile, far, own_mine, own_other, far_mine, far_other, work):
    count = tile.shape[0]
    my_row = lax.axis_index("prow")
    for index in range(count):
        place(work, PANELS + index, own_mine, own_other, index, tile, index)

    @pl.when(my_row < PANELS)
    def _():
        place(work, my_row, own_mine, own_other, 0, tile, 0)

    for number, group in enumerate(distance_groups(lax.axis_size("prow"))[0]):
        place_arrived(work, group, far_mine, far_other, number, far)

    def run(late, own):
        if late != 0:
            run_panel(work, 0, [index for index in range(1, PANELS) if index != late] + own)

    for_kinds(count, run)


def late_kernel(near, near_mine, near_other, given, out, work):
    del given
    size, count = work.shape[1], work.shape[0] - PANELS
    my_row, my_col = lax.axis_index("prow"), lax.axis_index("pcol")
    place_arrived(work, distance_groups(lax.axis_size("prow"))[1], near_mine, near_other, 0, near)

    def run(late, own):
        if late == 0:
            run_panel(work, 0, [*range(1, PANELS), *own])
        elif late is not None:
            run_panel(work, 0, [late], begin=False)
        for panel in range(1, PANELS):
            run_panel(work, panel, [*range(panel + 1, PANELS), *own])

    for_kinds(count, run)
    at = jnp.where(my_col < PANELS, my_col, PANELS)
    columns = pl.ds(pl.multiple_of(at * size, size), size)
    first = jnp.where(my_row < PANELS, my_row, PANELS)
    store(out, (0,), work[first, :, columns])
    for index in range(1, count):
        store(out, (index,), work[PANELS + index, :, columns])


def in_vmem(kernel, out_shapes, operands, spare=4, aliases={}):
    words = sum(operand.size for operand in operands) + sum(math.prod(shape) for shape in out_shapes)
    return pl.pallas_call(
        kernel,
        out_shape=[jax.ShapeDtypeStruct(shape, jnp.float32) for shape in out_shapes],
        in_specs=[pl.BlockSpec(memory_space=pltpu.VMEM)] * len(operands),
        out_specs=[pl.BlockSpec(memory_space=pltpu.VMEM)] * len(out_shapes),
        input_output_aliases=aliases,
        compiler_params=pltpu.CompilerParams(vmem_limit_bytes=4 * words + spare * 1024 * 1024),
    )(*operands)


def reverse(mask, chips):
    bits = chips.bit_length() - 1
    return sum(((mask >> bit) & 1) << (bits - 1 - bit) for bit in range(bits))


def pick_kernel(*refs):
    sources, mine = refs[:-1], refs[-1]
    chips = len(sources)
    me = lax.axis_index("pcol")
    even = lax.rem(me, 2) == 0
    for chip in range(chips):

        @pl.when(jnp.logical_and(me // 2 == chip, even))
        def _():
            mine[0] = sources[chip][...]
            mine[1] = sources[chip ^ 1][...]

        @pl.when(jnp.logical_and(me // 2 == chip, jnp.logical_not(even)))
        def _():
            mine[0] = sources[reverse(chip, chips)][...]


def arrivals(block):
    chips = lax.axis_size("pcol") // 2
    arrived = {0: block}

    def chip_of(column, mask):
        return column // 2 ^ (reverse(mask, chips) if column % 2 else mask)

    for mask in sorted(range(1, chips), key=lambda mask: (mask.bit_count(), -mask)):
        before = mask & (mask - 1)
        arrived[mask] = lax.ppermute(
            arrived[before],
            "pcol",
            [(2 * chip_of(c, before) + c % 2, 2 * chip_of(c, mask) + c % 2) for c in range(PANELS)],
        )
    return [arrived[mask] for mask in sorted(arrived)]


def exchange(arrived):
    (mine,) = in_vmem(pick_kernel, [(2, *arrived[0].shape)], arrived)
    other = lax.ppermute(mine, "pcol", [(c, c ^ 1) for c in range(lax.axis_size("pcol"))])
    return mine, other


def factored(matrix):
    shape = matrix.shape
    size = shape[4]
    tile = matrix.reshape(shape[0], shape[2] * size // LANES, LANES)
    row_count = lax.axis_size("prow")
    far_groups, near_group = distance_groups(row_count)

    def from_rows(block, group):
        total = None
        for d in group:
            arrived = lax.ppermute(block, "prow", [(k, (k + d) % row_count) for k in range(PANELS)])
            total = arrived if total is None else total + arrived
        return total

    rows = [from_rows(tile[:1], group) for group in far_groups]
    own = arrivals(tile)
    late, first = lax.optimization_barrier((tile[:1], rows[0]))
    near = from_rows(late, near_group)
    far = jnp.concatenate([first] + rows[1:])
    own = exchange(own)
    far_arrived = exchange(arrivals(far))
    near_arrived = exchange(arrivals(near))
    work = (PANELS + shape[0], size, (PANELS + 1) * size)
    (done,) = in_vmem(early_kernel, [work], [tile, far, *own, *far_arrived], 16)
    result, _ = in_vmem(late_kernel, [tile.shape, work], [near, *near_arrived, done], 16, {3: 1})
    return result.reshape(shape)


def solution(mesh):
    return jax.shard_map(
        factored,
        mesh=mesh,
        in_specs=(P(None, "prow", None, "pcol", None),),
        out_specs=P(None, "prow", None, "pcol", None),
        check_vma=False,
    )
```

time: 73.1 us -> 74.7 us (1.022)
  waiting for transfers between devices: 39.3 us -> 26.8 us
  starting transfers between devices: 25.1 us -> 36.9 us
  Pallas kernels: 6.93 us -> 8.08 us
  local copies, waits for them, and re-layouts: 1.24 us -> 2.28 us
    ppermute x3, starting transfers between devices: 10.9 us -> 25.1 us  [exchange(): lax.ppermute(mine, 'pcol', [(c, c ^ 1) for c in range(lax.axis_size('pcol...]
    ppermute x3, waiting for transfers between devices: 23.5 us -> 17.9 us  [from_rows(): lax.ppermute(block, 'prow', [(k, (k + d) % row_count) for k in range(PANE...]
    ppermute x9, waiting for transfers between devices: 14.2 us -> 8.91 us  [arrivals(): lax.ppermute(arrived[before], 'pcol', [(2 * chip_of(c, before) + c % 2, 2...]
    ppermute x9, starting transfers between devices: 10.3 us -> 7.98 us  [arrivals(): lax.ppermute(arrived[before], 'pcol', [(2 * chip_of(c, before) + c % 2, 2...]
    ppermute x3, waiting for transfers between devices: 1.54 us -> 0.01 us  [exchange(): lax.ppermute(mine, 'pcol', [(c, c ^ 1) for c in range(lax.axis_size('pcol...]
    pallas_call x4 -> x5, Pallas kernels: 6.93 us -> 8.08 us  [in_vmem(): pl.pallas_call(kernel, out_shape=[jax.ShapeDtypeStruct(shape, jnp.float32...]
    unnamed x3 -> x5, local copies, waits for them, and re-layouts: 0.02 us -> 1.06 us
  transfers between devices with their start and end apart: 15 -> 15, of which waited for: 8 -> 5; matrix products, arithmetic and copies ran while one was open for 0% -> 0% of each run, Pallas kernels for 0% -> 4%
where the time goes in v3:
time: 74.7 us; the launch traced here: 74.3 us
  starting transfers between devices  36.9 us (49%)
  waiting for transfers between devices  26.8 us (36%)
  Pallas kernels  8.08 us (11%)
  local copies, waits for them, and re-layouts  2.28 us (3%)
    ppermute x3, starting transfers between devices, exchange(): lax.ppermute(mine, 'pcol', [(c, c ^ 1) for c in range(lax.axis_size('pcol...  25.1 us
    ppermute x3, waiting for transfers between devices, from_rows(): lax.ppermute(block, 'prow', [(k, (k + d) % row_count) for k in range(PANE...  17.9 us
    ppermute x9, waiting for transfers between devices, arrivals(): lax.ppermute(arrived[before], 'pcol', [(2 * chip_of(c, before) + c % 2, 2...  8.91 us
    pallas_call x5, Pallas kernels, in_vmem(): pl.pallas_call(kernel, out_shape=[jax.ShapeDtypeStruct(shape, jnp.float32...  8.08 us
    ppermute x9, starting transfers between devices, arrivals(): lax.ppermute(arrived[before], 'pcol', [(2 * chip_of(c, before) + c % 2, 2...  7.98 us
    ppermute x3, starting transfers between devices, from_rows(): lax.ppermute(block, 'prow', [(k, (k + d) % row_count) for k in range(PANE...  3.88 us
  transfers between devices with their start and end apart: 15, of which 5 were waited for; matrix products, arithmetic and copies ran while one was open for 0% of the time, Pallas kernels for 4%

profile of v3, /device:TPU:29, one launch (start us, length us, event | category | flops | bytes accessed | tf_op | source)
XLA Modules:
  0.0 74.3 jit_solution(5766398110839236894)
XLA Ops:
  0.0 0.0 copy-start.1
  0.0 1.2 %slice.8 = f32[1,1,256,1,256]{4,3,2,1,0:T(1,128)S(1)} slice(f32[2,1,256,1,256]{4,3,2,1,0:T(1,128)} %param.1), slice={[0:1], [0:1], [0:256], [0:1], [0:256]} | slice | bytes 524288 | tf_op jit(solution)/shard_map/slice | solution.py:251
  1.2 1.3 %collective-permute-start = (f32[1,512,128]{2,1,0:T(8,128)S(1)}, f32[1,512,128]{2,1,0:T(8,128)S(1)}, u32[]{:S(2)}, u32[]{:S(2)}) collective-permute-start(f32[1,512,128]{2,1,0:T(8,128)S(1)} %bitcast.7), channel_id=1, source_target_pairs={{0,8},{8,16},{16,24},{1,9},{9,17},{17,25},{2,10},{10,18},{18,26},{... | collective-permute-start | bytes 786440 | tf_op jit(solution)/shard_map/ppermute | solution.py:245
  2.5 1.3 %collective-permute-start.6 = (f32[1,512,128]{2,1,0:T(8,128)S(1)}, f32[1,512,128]{2,1,0:T(8,128)S(1)}, u32[]{:S(2)}, u32[]{:S(2)}) collective-permute-start(f32[1,512,128]{2,1,0:T(8,128)S(1)} %bitcast.8), channel_id=1, source_target_pairs={{0,24},{8,0},{16,8},{1,25},{9,1},{17,9},{2,26},{10,2},{18,10},{3,2... | collective-permute-start | bytes 786440 | tf_op jit(solution)/shard_map/ppermute | solution.py:245
  3.8 0.7 collective-permute-start.8
  4.5 6.0 %collective-permute-done = f32[1,512,128]{2,1,0:T(8,128)S(1)} collective-permute-done((f32[1,512,128]{2,1,0:T(8,128)S(1)}, f32[1,512,128]{2,1,0:T(8,128)S(1)}, u32[]{:S(2)}, u32[]{:S(2)}) %collective-permute-start) | collective-permute-done | bytes 262176 | tf_op jit(solution)/shard_map/ppermute | solution.py:245
  10.5 5.2 %collective-permute-done.6 = f32[1,512,128]{2,1,0:T(8,128)S(1)} collective-permute-done((f32[1,512,128]{2,1,0:T(8,128)S(1)}, f32[1,512,128]{2,1,0:T(8,128)S(1)}, u32[]{:S(2)}, u32[]{:S(2)}) %collective-permute-start.6) | collective-permute-done | bytes 262176 | tf_op jit(solution)/shard_map/ppermute | solution.py:245
  15.8 0.7 collective-permute-start.12
  16.5 1.3 %collective-permute-start.7 = (f32[2,512,128]{2,1,0:T(8,128)}, f32[2,512,128]{2,1,0:T(8,128)S(1)}, u32[]{:S(2)}, u32[]{:S(2)}) collective-permute-start(f32[2,512,128]{2,1,0:T(8,128)} %bitcast.4), channel_id=1, source_target_pairs={{0,2},{1,5},{2,0},{8,10},{9,13},{10,8},{16,18},{17,21},{18,16},{24... | collective-permute-start | bytes 1572872 | tf_op jit(solution)/shard_map/ppermute | solution.py:221
  17.8 0.0 collective-permute-done.8.refs_2_
  17.8 0.7 collective-permute-start.9
  18.5 1.3 %collective-permute-start.11 = (f32[2,512,128]{2,1,0:T(8,128)S(1)}, f32[2,512,128]{2,1,0:T(8,128)S(1)}, u32[]{:S(2)}, u32[]{:S(2)}) collective-permute-start(f32[2,512,128]{2,1,0:T(8,128)S(1)} %constant_dynamic-update-slice_fusion.refs_0_.far), channel_id=1, source_target_pairs={{0,2},{1,5},{2,0},{8,10},{9,13},{10,8},{16,18},{17,21},{18,16},{24... | collective-permute-start | bytes 1572872 | tf_op jit(solution)/shard_map/ppermute | solution.py:221
  19.8 0.0 collective-permute-done.12.refs_2_
  19.8 0.7 collective-permute-start.13
  20.5 1.3 %collective-permute-start.1 = (f32[1,512,128]{2,1,0:T(8,128)S(1)}, f32[1,512,128]{2,1,0:T(8,128)S(1)}, u32[]{:S(2)}, u32[]{:S(2)}) collective-permute-start(f32[1,512,128]{2,1,0:T(8,128)S(1)} %bitcast.9), channel_id=1, source_target_pairs={{0,16},{8,24},{16,0},{1,17},{9,25},{17,1},{2,18},{10,26},{18,2},{3... | collective-permute-start | bytes 786440 | tf_op jit(solution)/shard_map/ppermute | solution.py:245
  21.8 6.7 %collective-permute-done.1.refs_0_.near = f32[1,512,128]{2,1,0:T(8,128)S(1)} collective-permute-done((f32[1,512,128]{2,1,0:T(8,128)S(1)}, f32[1,512,128]{2,1,0:T(8,128)S(1)}, u32[]{:S(2)}, u32[]{:S(2)}) %collective-permute-start.1) | collective-permute-done | bytes 262176 | tf_op jit(solution)/shard_map/ppermute | solution.py:245
  28.5 0.7 collective-permute-start.3
  29.2 3.2 %collective-permute-done.7.refs_1_ = f32[2,512,128]{2,1,0:T(8,128)S(1)} collective-permute-done((f32[2,512,128]{2,1,0:T(8,128)}, f32[2,512,128]{2,1,0:T(8,128)S(1)}, u32[]{:S(2)}, u32[]{:S(2)}) %collective-permute-start.7) | collective-permute-done | bytes 524320 | tf_op jit(solution)/shard_map/ppermute | solution.py:221
  32.4 0.0 collective-permute-done.9.refs_3_
  32.4 0.0 copy-start
  32.4 1.0 %copy-done = f32[2,1,256,1,256]{4,3,2,1,0:T(1,128)S(1)} copy-done((f32[2,1,256,1,256]{4,3,2,1,0:T(1,128)S(1)}, f32[2,1,256,1,256]{4,3,2,1,0:T(1,128)}, u32[]{:S(2)}) %copy-start) | copy-done | bytes 524312
  33.5 18.5 %collective-permute-start.10 = (f32[2,2,512,128]{3,2,1,0:T(8,128)S(1)}, f32[2,2,512,128]{3,2,1,0:T(8,128)S(1)}, u32[]{:S(2)}, u32[]{:S(2)}) collective-permute-start(f32[2,2,512,128]{3,2,1,0:T(8,128)S(1)} %shard_map.18.own_mine), channel_id=1, source_target_pairs={{0,1},{1,0},{2,3},{3,2},{4,5},{5,4},{6,7},{7,6},{8,9},{9,8},{10,11... | collective-permute-start | bytes 3145736 | tf_op jit(solution)/shard_map/ppermute | solution.py:231
  52.0 0.0 collective-permute-done.11.refs_1_
  52.0 0.0 collective-permute-done.13.refs_3_
  52.0 0.2 collective-permute-start.14
  52.2 1.3 %collective-permute-start.2 = (f32[1,512,128]{2,1,0:T(8,128)S(1)}, f32[1,512,128]{2,1,0:T(8,128)S(1)}, u32[]{:S(2)}, u32[]{:S(2)}) collective-permute-start(f32[1,512,128]{2,1,0:T(8,128)S(1)} %collective-permute-done.1.refs_0_.near), channel_id=1, source_target_pairs={{0,2},{1,5},{2,0},{8,10},{9,13},{10,8},{16,18},{17,21},{18,16},{24... | collective-permute-start | bytes 786440 | tf_op jit(solution)/shard_map/ppermute | solution.py:221
  53.5 0.0 collective-permute-done.3.refs_2_
  53.5 0.7 collective-permute-start.4
  54.2 5.7 %collective-permute-done.2.refs_1_ = f32[1,512,128]{2,1,0:T(8,128)S(1)} collective-permute-done((f32[1,512,128]{2,1,0:T(8,128)S(1)}, f32[1,512,128]{2,1,0:T(8,128)S(1)}, u32[]{:S(2)}, u32[]{:S(2)}) %collective-permute-start.2) | collective-permute-done | bytes 262176 | tf_op jit(solution)/shard_map/ppermute | solution.py:221
  59.8 0.0 collective-permute-done.4.refs_3_
  59.9 6.4 %collective-permute-start.5 = (f32[2,1,512,128]{3,2,1,0:T(8,128)S(1)}, f32[2,1,512,128]{3,2,1,0:T(8,128)S(1)}, u32[]{:S(2)}, u32[]{:S(2)}) collective-permute-start(f32[2,1,512,128]{3,2,1,0:T(8,128)S(1)} %shard_map.17.near_mine), channel_id=1, source_target_pairs={{0,1},{1,0},{2,3},{3,2},{4,5},{5,4},{6,7},{7,6},{8,9},{9,8},{10,11... | collective-permute-start | bytes 1572872 | tf_op jit(solution)/shard_map/ppermute | solution.py:231
  66.3 0.0 collective-permute-done.10.own_other
  66.3 0.0 collective-permute-done.14.far_other
  66.3 0.0 copy-done.1
  66.3 3.0 %shard_map.20.given = f32[5,256,1024]{2,1,0:T(8,128)S(1)} custom-call(f32[2,512,128]{2,1,0:T(8,128)S(1)} %bitcast.6, f32[2,512,128]{2,1,0:T(8,128)S(1)} %constant_dynamic-update-slice_fusion.refs_0_.far, f32[2,2,512,128]{3,2,1,0:T(8,128)S(1)} %shard_map.18.own_mine, f32[2,2,512,128]{3,2,1,0:T(8,128)S(1)} %collective-permute-done.10.own_other, ...), custom_call_target="tpu_custom_call" | custom-call | tf_op jit(solution)/shard_map/pallas_call | solution.py:180
  69.3 0.0 collective-permute-done.5.near_other
  69.3 5.0 %shard_map.21 = (f32[2,512,128]{2,1,0:T(8,128)}, f32[5,256,1024]{2,1,0:T(8,128)S(1)}) custom-call(f32[1,512,128]{2,1,0:T(8,128)S(1)} %collective-permute-done.1.refs_0_.near, f32[2,1,512,128]{3,2,1,0:T(8,128)S(1)} %shard_map.17.near_mine, f32[2,1,512,128]{3,2,1,0:T(8,128)S(1)} %collective-permute-done.5.near_other, ...), custom_call_target="tpu_custom_call", output_to_operand_aliasing={{1}: (3, {})} | custom-call | tf_op jit(solution)/shard_map/pallas_call | solution.py:180
  (5 shorter events, 0.1 us)
Async XLA Ops:
  0.0 66.3 %copy-start.1 = (f32[2,1,256,1,256]{4,3,2,1,0:T(1,128)S(1)}, f32[2,1,256,1,256]{4,3,2,1,0:T(1,128)}, u32[]{:S(2)}) copy-start(f32[2,1,256,1,256]{4,3,2,1,0:T(1,128)} %param.1) | copy-start | bytes 1572868
  1.2 9.3 %collective-permute-start = (f32[1,512,128]{2,1,0:T(8,128)S(1)}, f32[1,512,128]{2,1,0:T(8,128)S(1)}, u32[]{:S(2)}, u32[]{:S(2)}) collective-permute-start(f32[1,512,128]{2,1,0:T(8,128)S(1)} %bitcast.7), channel_id=1, source_target_pairs={{0,8},{8,16},{16,24},{1,9},{9,17},{17,25},{2,10},{10,18},{18,26},{... | collective-permute-start | bytes 786440 | tf_op jit(solution)/shard_map/ppermute | solution.py:245
  2.5 13.2 %collective-permute-start.6 = (f32[1,512,128]{2,1,0:T(8,128)S(1)}, f32[1,512,128]{2,1,0:T(8,128)S(1)}, u32[]{:S(2)}, u32[]{:S(2)}) collective-permute-start(f32[1,512,128]{2,1,0:T(8,128)S(1)} %bitcast.8), channel_id=1, source_target_pairs={{0,24},{8,0},{16,8},{1,25},{9,1},{17,9},{2,26},{10,2},{18,10},{3,2... | collective-permute-start | bytes 786440 | tf_op jit(solution)/shard_map/ppermute | solution.py:245
  3.8 13.9 %collective-permute-start.8 = (f32[2,512,128]{2,1,0:T(8,128)}, f32[2,512,128]{2,1,0:T(8,128)S(1)}, u32[]{:S(2)}, u32[]{:S(2)}) collective-permute-start(f32[2,512,128]{2,1,0:T(8,128)} %bitcast.3), channel_id=1, source_target_pairs={{0,4},{1,3},{2,6},{8,12},{9,11},{10,14},{16,20},{17,19},{18,22},{2... | collective-permute-start | bytes 1572872 | tf_op jit(solution)/shard_map/ppermute | solution.py:221
  15.8 4.0 %collective-permute-start.12 = (f32[2,512,128]{2,1,0:T(8,128)S(1)}, f32[2,512,128]{2,1,0:T(8,128)S(1)}, u32[]{:S(2)}, u32[]{:S(2)}) collective-permute-start(f32[2,512,128]{2,1,0:T(8,128)S(1)} %constant_dynamic-update-slice_fusion.refs_0_.far), channel_id=1, source_target_pairs={{0,4},{1,3},{2,6},{8,12},{9,11},{10,14},{16,20},{17,19},{18,22},{2... | collective-permute-start | bytes 1572872 | tf_op jit(solution)/shard_map/ppermute | solution.py:221
  16.5 16.0 %collective-permute-start.7 = (f32[2,512,128]{2,1,0:T(8,128)}, f32[2,512,128]{2,1,0:T(8,128)S(1)}, u32[]{:S(2)}, u32[]{:S(2)}) collective-permute-start(f32[2,512,128]{2,1,0:T(8,128)} %bitcast.4), channel_id=1, source_target_pairs={{0,2},{1,5},{2,0},{8,10},{9,13},{10,8},{16,18},{17,21},{18,16},{24... | collective-permute-start | bytes 1572872 | tf_op jit(solution)/shard_map/ppermute | solution.py:221
  17.8 14.6 %collective-permute-start.9 = (f32[2,512,128]{2,1,0:T(8,128)S(1)}, f32[2,512,128]{2,1,0:T(8,128)S(1)}, u32[]{:S(2)}, u32[]{:S(2)}) collective-permute-start(f32[2,512,128]{2,1,0:T(8,128)S(1)} %collective-permute-done.8.refs_2_), channel_id=1, source_target_pairs={{4,6},{3,7},{6,4},{12,14},{11,15},{14,12},{20,22},{19,23},{22,20},... | collective-permute-start | bytes 1572872 | tf_op jit(solution)/shard_map/ppermute | solution.py:221
  18.5 33.5 %collective-permute-start.11 = (f32[2,512,128]{2,1,0:T(8,128)S(1)}, f32[2,512,128]{2,1,0:T(8,128)S(1)}, u32[]{:S(2)}, u32[]{:S(2)}) collective-permute-start(f32[2,512,128]{2,1,0:T(8,128)S(1)} %constant_dynamic-update-slice_fusion.refs_0_.far), channel_id=1, source_target_pairs={{0,2},{1,5},{2,0},{8,10},{9,13},{10,8},{16,18},{17,21},{18,16},{24... | collective-permute-start | bytes 1572872 | tf_op jit(solution)/shard_map/ppermute | solution.py:221
  19.8 32.2 %collective-permute-start.13 = (f32[2,512,128]{2,1,0:T(8,128)S(1)}, f32[2,512,128]{2,1,0:T(8,128)S(1)}, u32[]{:S(2)}, u32[]{:S(2)}) collective-permute-start(f32[2,512,128]{2,1,0:T(8,128)S(1)} %collective-permute-done.12.refs_2_), channel_id=1, source_target_pairs={{4,6},{3,7},{6,4},{12,14},{11,15},{14,12},{20,22},{19,23},{22,20},... | collective-permute-start | bytes 1572872 | tf_op jit(solution)/shard_map/ppermute | solution.py:221
  20.5 8.0 %collective-permute-start.1 = (f32[1,512,128]{2,1,0:T(8,128)S(1)}, f32[1,512,128]{2,1,0:T(8,128)S(1)}, u32[]{:S(2)}, u32[]{:S(2)}) collective-permute-start(f32[1,512,128]{2,1,0:T(8,128)S(1)} %bitcast.9), channel_id=1, source_target_pairs={{0,16},{8,24},{16,0},{1,17},{9,25},{17,1},{2,18},{10,26},{18,2},{3... | collective-permute-start | bytes 786440 | tf_op jit(solution)/shard_map/ppermute | solution.py:245
  28.5 25.0 %collective-permute-start.3 = (f32[1,512,128]{2,1,0:T(8,128)S(1)}, f32[1,512,128]{2,1,0:T(8,128)S(1)}, u32[]{:S(2)}, u32[]{:S(2)}) collective-permute-start(f32[1,512,128]{2,1,0:T(8,128)S(1)} %collective-permute-done.1.refs_0_.near), channel_id=1, source_target_pairs={{0,4},{1,3},{2,6},{8,12},{9,11},{10,14},{16,20},{17,19},{18,22},{2... | collective-permute-start | bytes 786440 | tf_op jit(solution)/shard_map/ppermute | solution.py:221
  32.4 1.0 %copy-start = (f32[2,1,256,1,256]{4,3,2,1,0:T(1,128)S(1)}, f32[2,1,256,1,256]{4,3,2,1,0:T(1,128)}, u32[]{:S(2)}) copy-start(f32[2,1,256,1,256]{4,3,2,1,0:T(1,128)} %param.1) | copy-start | bytes 1572868
  33.5 32.8 %collective-permute-start.10 = (f32[2,2,512,128]{3,2,1,0:T(8,128)S(1)}, f32[2,2,512,128]{3,2,1,0:T(8,128)S(1)}, u32[]{:S(2)}, u32[]{:S(2)}) collective-permute-start(f32[2,2,512,128]{3,2,1,0:T(8,128)S(1)} %shard_map.18.own_mine), channel_id=1, source_target_pairs={{0,1},{1,0},{2,3},{3,2},{4,5},{5,4},{6,7},{7,6},{8,9},{9,8},{10,11... | collective-permute-start | bytes 3145736 | tf_op jit(solution)/shard_map/ppermute | solution.py:231
  52.0 14.3 %collective-permute-start.14 = (f32[2,2,512,128]{3,2,1,0:T(8,128)S(1)}, f32[2,2,512,128]{3,2,1,0:T(8,128)S(1)}, u32[]{:S(2)}, u32[]{:S(2)}) collective-permute-start(f32[2,2,512,128]{3,2,1,0:T(8,128)S(1)} %shard_map.19.far_mine), channel_id=1, source_target_pairs={{0,1},{1,0},{2,3},{3,2},{4,5},{5,4},{6,7},{7,6},{8,9},{9,8},{10,11... | collective-permute-start | bytes 3145736 | tf_op jit(solution)/shard_map/ppermute | solution.py:231
  52.2 7.6 %collective-permute-start.2 = (f32[1,512,128]{2,1,0:T(8,128)S(1)}, f32[1,512,128]{2,1,0:T(8,128)S(1)}, u32[]{:S(2)}, u32[]{:S(2)}) collective-permute-start(f32[1,512,128]{2,1,0:T(8,128)S(1)} %collective-permute-done.1.refs_0_.near), channel_id=1, source_target_pairs={{0,2},{1,5},{2,0},{8,10},{9,13},{10,8},{16,18},{17,21},{18,16},{24... | collective-permute-start | bytes 786440 | tf_op jit(solution)/shard_map/ppermute | solution.py:221
  53.5 6.3 %collective-permute-start.4 = (f32[1,512,128]{2,1,0:T(8,128)S(1)}, f32[1,512,128]{2,1,0:T(8,128)S(1)}, u32[]{:S(2)}, u32[]{:S(2)}) collective-permute-start(f32[1,512,128]{2,1,0:T(8,128)S(1)} %collective-permute-done.3.refs_2_), channel_id=1, source_target_pairs={{4,6},{3,7},{6,4},{12,14},{11,15},{14,12},{20,22},{19,23},{22,20},... | collective-permute-start | bytes 786440 | tf_op jit(solution)/shard_map/ppermute | solution.py:221
  59.9 9.4 %collective-permute-start.5 = (f32[2,1,512,128]{3,2,1,0:T(8,128)S(1)}, f32[2,1,512,128]{3,2,1,0:T(8,128)S(1)}, u32[]{:S(2)}, u32[]{:S(2)}) collective-permute-start(f32[2,1,512,128]{3,2,1,0:T(8,128)S(1)} %shard_map.17.near_mine), channel_id=1, source_target_pairs={{0,1},{1,0},{2,3},{3,2},{4,5},{5,4},{6,7},{7,6},{8,9},{9,8},{10,11... | collective-permute-start | bytes 1572872 | tf_op jit(solution)/shard_map/ppermute | solution.py:231

commit v4 on v3

--- a/solution.py
+++ b/solution.py
@@ -65,10 +65,15 @@
         ref[(*index, pl.ds(part, size, stride=step), slice(None))] = value[:, part * LANES : (part + 1) * LANES]
 
 
+def comes_late(row, plane, row_count):
+    distance = (plane - row) % row_count
+    return distance in distance_groups(row_count)[1] and (distance != 2 or row + 2 < row_count)
+
+
 def plane_kinds(row_count):
     kinds = {}
     for plane in range(row_count):
-        late = [k for k in range(PANELS) if (plane - k) % row_count in distance_groups(row_count)[1]]
+        late = [k for k in range(PANELS) if comes_late(k, plane, row_count)]
         kinds.setdefault((late[0] if late else None, plane < PANELS), []).append(plane)
     return kinds
 
@@ -95,12 +100,15 @@
         work[target, :, column(2, size)] = load(other, (1, piece), size)
 
 
-def place_arrived(work, group, mine, other, piece, own):
+def place_arrived(work, group, mine, other, piece, own, late):
     my_row, row_count = lax.axis_index("prow"), lax.axis_size("prow")
     for distance in group:
         source = lax.rem(my_row + row_count - distance, row_count)
-
-        @pl.when(source < PANELS)
+        here = source < PANELS
+        if distance == 2:
+            here = jnp.logical_and(here, (source + 2 < row_count) == late)
+
+        @pl.when(here)
         def _():
             place(work, source, mine, other, piece, own, piece)
 
@@ -143,7 +151,7 @@
         place(work, my_row, own_mine, own_other, 0, tile, 0)
 
     for number, group in enumerate(distance_groups(lax.axis_size("prow"))[0]):
-        place_arrived(work, group, far_mine, far_other, number, far)
+        place_arrived(work, group + [2] * (number == 0), far_mine, far_other, number, far, False)
 
     def run(late, own):
         if late != 0:
@@ -156,7 +164,7 @@
     del given
     size, count = work.shape[1], work.shape[0] - PANELS
     my_row, my_col = lax.axis_index("prow"), lax.axis_index("pcol")
-    place_arrived(work, distance_groups(lax.axis_size("prow"))[1], near_mine, near_other, 0, near)
+    place_arrived(work, distance_groups(lax.axis_size("prow"))[1], near_mine, near_other, 0, near, True)
 
     def run(late, own):
         if late == 0:
@@ -209,7 +217,7 @@
             mine[0] = sources[reverse(chip, chips)][...]
 
 
-def arrivals(block):
+def arrivals(block, planes):
     chips = lax.axis_size("pcol") // 2
     arrived = {0: block}
 
@@ -218,10 +226,11 @@
 
     for mask in sorted(range(1, chips), key=lambda mask: (mask.bit_count(), -mask)):
         before = mask & (mask - 1)
+        pairs = [(2 * chip_of(c, before) + c % 2, 2 * chip_of(c, mask) + c % 2) for c in range(PANELS)]
         arrived[mask] = lax.ppermute(
             arrived[before],
-            "pcol",
-            [(2 * chip_of(c, before) + c % 2, 2 * chip_of(c, mask) + c % 2) for c in range(PANELS)],
+            ("prow", "pcol"),
+            [(p * 2 * chips + a, p * 2 * chips + b) for p in planes for a, b in pairs],
         )
     return [arrived[mask] for mask in sorted(arrived)]
 
@@ -239,21 +248,29 @@
     row_count = lax.axis_size("prow")
     far_groups, near_group = distance_groups(row_count)
 
-    def from_rows(block, group):
-        total = None
-        for d in group:
-            arrived = lax.ppermute(block, "prow", [(k, (k + d) % row_count) for k in range(PANELS)])
-            total = arrived if total is None else total + arrived
-        return total
-
-    rows = [from_rows(tile[:1], group) for group in far_groups]
-    own = arrivals(tile)
-    late, first = lax.optimization_barrier((tile[:1], rows[0]))
-    near = from_rows(late, near_group)
-    far = jnp.concatenate([first] + rows[1:])
-    own = exchange(own)
-    far_arrived = exchange(arrivals(far))
-    near_arrived = exchange(arrivals(near))
+    def from_rows(block, pairs):
+        return lax.ppermute(block, "prow", pairs)
+
+    def total(parts):
+        return functools.reduce(jnp.add, parts)
+
+    def direct(d):
+        return from_rows(tile[:1], [(k, (k + d) % row_count) for k in range(PANELS)])
+
+    next_row = direct(1)
+    rows = [[direct(d) for d in group if d != 1] for group in far_groups]
+    rows[0].append(next_row)
+    wrapped = [(k, (k + 2) % row_count) for k in range(PANELS) if k + 2 >= row_count]
+    if wrapped:
+        rows[0].append(from_rows(tile[:1], wrapped))
+    far = jnp.concatenate([total(parts) for parts in rows])
+    passed = from_rows(next_row, [(k + 1, k + 2) for k in range(PANELS) if k + 2 < row_count])
+    near = total([passed] + [direct(d) for d in near_group if d != 2])
+    every = range(row_count)
+    late_planes = [p for p in every if any(comes_late(k, p, row_count) for k in range(PANELS))]
+    own = exchange(arrivals(tile, every))
+    far_arrived = exchange(arrivals(far, every))
+    near_arrived = exchange(arrivals(near, late_planes))
     work = (PANELS + shape[0], size, (PANELS + 1) * size)
     (done,) = in_vmem(early_kernel, [work], [tile, far, *own, *far_arrived], 16)
     result, _ = in_vmem(late_kernel, [tile.shape, work], [near, *near_arrived, done], 16, {3: 1})

time: 74.7 us -> 72.4 us (0.969)
  the two profiles are of different devices: /device:TPU:29 before, /device:TPU:21 now
where the time goes in v4:
time: 72.4 us; the launch traced here: 72 us
  starting transfers between devices  48.8 us (67%)
  waiting for transfers between devices  14.6 us (20%)
  Pallas kernels  6.16 us (9%)
  local copies, waits for them, and re-layouts  2.25 us (3%)
    ppermute x3, starting transfers between devices, exchange(): lax.ppermute(mine, 'pcol', [(c, c ^ 1) for c in range(lax.axis_size('pcol...  27.4 us
    ppermute x4, starting transfers between devices, from_rows(): return lax.ppermute(block, 'prow', pairs)  13.4 us
    ppermute x9, starting transfers between devices, arrivals(): lax.ppermute(arrived[before], ('prow', 'pcol'), [(p * 2 * chips + a, p *...  7.98 us
    ppermute x4, waiting for transfers between devices, from_rows(): return lax.ppermute(block, 'prow', pairs)  7.56 us
    pallas_call x5, Pallas kernels, in_vmem(): pl.pallas_call(kernel, out_shape=[jax.ShapeDtypeStruct(shape, jnp.float32...  6.16 us
    ppermute x9, waiting for transfers between devices, arrivals(): lax.ppermute(arrived[before], ('prow', 'pcol'), [(p * 2 * chips + a, p *...  5.79 us
  transfers between devices with their start and end apart: 16, of which 6 were waited for; matrix products, arithmetic and copies ran while one was open for 0% of the time, Pallas kernels for 1%

profile of v4, /device:TPU:21, one launch (start us, length us, event | category | flops | bytes accessed | tf_op | source)
XLA Modules:
  0.0 72.0 jit_solution(6766315144356975085)
XLA Ops:
  0.0 0.0 copy-start.1
  0.0 1.2 %slice.8 = f32[1,1,256,1,256]{4,3,2,1,0:T(1,128)S(1)} slice(f32[2,1,256,1,256]{4,3,2,1,0:T(1,128)} %param.1), slice={[0:1], [0:1], [0:256], [0:1], [0:256]} | slice | bytes 524288 | tf_op jit(solution)/shard_map/slice | solution.py:258
  1.2 2.0 %collective-permute-start.6 = (f32[1,512,128]{2,1,0:T(8,128)S(1)}, f32[1,512,128]{2,1,0:T(8,128)S(1)}, u32[]{:S(2)}, u32[]{:S(2)}) collective-permute-start(f32[1,512,128]{2,1,0:T(8,128)S(1)} %bitcast.7), channel_id=1, source_target_pairs={{16,0},{17,1},{18,2},{19,3},{20,4},{21,5},{22,6},{23,7}} | collective-permute-start | bytes 786440 | tf_op jit(solution)/shard_map/ppermute | solution.py:252
  3.2 1.9 %collective-permute-start = (f32[1,512,128]{2,1,0:T(8,128)S(1)}, f32[1,512,128]{2,1,0:T(8,128)S(1)}, u32[]{:S(2)}, u32[]{:S(2)}) collective-permute-start(f32[1,512,128]{2,1,0:T(8,128)S(1)} %bitcast.8), channel_id=1, source_target_pairs={{0,8},{8,16},{16,24},{1,9},{9,17},{17,25},{2,10},{10,18},{18,26},{... | collective-permute-start | bytes 786440 | tf_op jit(solution)/shard_map/ppermute | solution.py:252
  5.1 3.4 %collective-permute-start.7 = (f32[1,512,128]{2,1,0:T(8,128)S(1)}, f32[1,512,128]{2,1,0:T(8,128)S(1)}, u32[]{:S(2)}, u32[]{:S(2)}) collective-permute-start(f32[1,512,128]{2,1,0:T(8,128)S(1)} %bitcast.9), channel_id=1, source_target_pairs={{0,24},{8,0},{16,8},{1,25},{9,1},{17,9},{2,26},{10,2},{18,10},{3,2... | collective-permute-start | bytes 786440 | tf_op jit(solution)/shard_map/ppermute | solution.py:252
  8.5 0.7 collective-permute-start.9
  9.2 0.0 collective-permute-done.6
  9.2 3.9 %collective-permute-done = f32[1,512,128]{2,1,0:T(8,128)S(1)} collective-permute-done((f32[1,512,128]{2,1,0:T(8,128)S(1)}, f32[1,512,128]{2,1,0:T(8,128)S(1)}, u32[]{:S(2)}, u32[]{:S(2)}) %collective-permute-start) | collective-permute-done | bytes 262176 | tf_op jit(solution)/shard_map/ppermute | solution.py:252
  13.2 0.4 collective-permute-done.7
  13.6 0.7 collective-permute-start.13
  14.3 1.3 %collective-permute-start.8 = (f32[2,512,128]{2,1,0:T(8,128)}, f32[2,512,128]{2,1,0:T(8,128)S(1)}, u32[]{:S(2)}, u32[]{:S(2)}) collective-permute-start(f32[2,512,128]{2,1,0:T(8,128)} %bitcast.4), channel_id=1, source_target_pairs={{0,2},{1,5},{2,0},{8,10},{9,13},{10,8},{16,18},{17,21},{18,16},{24... | collective-permute-start | bytes 1572872 | tf_op jit(solution)/shard_map/ppermute | solution.py:230
  15.6 0.0 collective-permute-done.9.refs_2_
  15.6 0.7 collective-permute-start.10
  16.3 1.3 %collective-permute-start.12 = (f32[2,512,128]{2,1,0:T(8,128)S(1)}, f32[2,512,128]{2,1,0:T(8,128)S(1)}, u32[]{:S(2)}, u32[]{:S(2)}) collective-permute-start(f32[2,512,128]{2,1,0:T(8,128)S(1)} %pad_maximum_fusion.refs_0_.far), channel_id=1, source_target_pairs={{0,2},{1,5},{2,0},{8,10},{9,13},{10,8},{16,18},{17,21},{18,16},{24... | collective-permute-start | bytes 1572872 | tf_op jit(solution)/shard_map/ppermute | solution.py:230
  17.6 0.0 collective-permute-done.13.refs_2_
  17.6 0.7 collective-permute-start.14
  18.3 6.1 %collective-permute-start.1 = (f32[1,512,128]{2,1,0:T(8,128)S(1)}, f32[1,512,128]{2,1,0:T(8,128)S(1)}, u32[]{:S(2)}, u32[]{:S(2)}) collective-permute-start(f32[1,512,128]{2,1,0:T(8,128)S(1)} %collective-permute-done), channel_id=1, source_target_pairs={{8,16},{16,24},{9,17},{17,25},{10,18},{18,26},{11,19},{19,27},{12,... | collective-permute-start | bytes 786440 | tf_op jit(solution)/shard_map/ppermute | solution.py:252
  24.4 3.3 %collective-permute-done.1.refs_0_.near = f32[1,512,128]{2,1,0:T(8,128)S(1)} collective-permute-done((f32[1,512,128]{2,1,0:T(8,128)S(1)}, f32[1,512,128]{2,1,0:T(8,128)S(1)}, u32[]{:S(2)}, u32[]{:S(2)}) %collective-permute-start.1) | collective-permute-done | bytes 262176 | tf_op jit(solution)/shard_map/ppermute | solution.py:252
  27.7 0.7 collective-permute-start.3
  28.4 0.1 collective-permute-done.8.refs_1_
  28.5 0.0 collective-permute-done.10.refs_3_
  28.5 0.0 copy-start
  28.5 1.0 %copy-done = f32[2,1,256,1,256]{4,3,2,1,0:T(1,128)S(1)} copy-done((f32[2,1,256,1,256]{4,3,2,1,0:T(1,128)S(1)}, f32[2,1,256,1,256]{4,3,2,1,0:T(1,128)}, u32[]{:S(2)}) %copy-start) | copy-done | bytes 524312
  29.6 20.8 %collective-permute-start.11 = (f32[2,2,512,128]{3,2,1,0:T(8,128)S(1)}, f32[2,2,512,128]{3,2,1,0:T(8,128)S(1)}, u32[]{:S(2)}, u32[]{:S(2)}) collective-permute-start(f32[2,2,512,128]{3,2,1,0:T(8,128)S(1)} %shard_map.18.own_mine), channel_id=1, source_target_pairs={{0,1},{1,0},{2,3},{3,2},{4,5},{5,4},{6,7},{7,6},{8,9},{9,8},{10,11... | collective-permute-start | bytes 3145736 | tf_op jit(solution)/shard_map/ppermute | solution.py:240
  50.4 0.0 collective-permute-done.12.refs_1_
  50.4 0.0 collective-permute-done.14.refs_3_
  50.4 0.2 collective-permute-start.15
  50.6 1.3 %collective-permute-start.2 = (f32[1,512,128]{2,1,0:T(8,128)S(1)}, f32[1,512,128]{2,1,0:T(8,128)S(1)}, u32[]{:S(2)}, u32[]{:S(2)}) collective-permute-start(f32[1,512,128]{2,1,0:T(8,128)S(1)} %collective-permute-done.1.refs_0_.near), channel_id=1, source_target_pairs={{16,18},{17,21},{18,16},{24,26},{25,29},{26,24}} | collective-permute-start | bytes 786440 | tf_op jit(solution)/shard_map/ppermute | solution.py:230
  51.9 0.0 collective-permute-done.3.refs_2_
  51.9 0.7 collective-permute-start.4
  52.6 5.7 %collective-permute-done.2.refs_1_ = f32[1,512,128]{2,1,0:T(8,128)S(1)} collective-permute-done((f32[1,512,128]{2,1,0:T(8,128)S(1)}, f32[1,512,128]{2,1,0:T(8,128)S(1)}, u32[]{:S(2)}, u32[]{:S(2)}) %collective-permute-start.2) | collective-permute-done | bytes 262176 | tf_op jit(solution)/shard_map/ppermute | solution.py:230
  58.2 0.0 collective-permute-done.4.refs_3_
  58.3 6.4 %collective-permute-start.5 = (f32[2,1,512,128]{3,2,1,0:T(8,128)S(1)}, f32[2,1,512,128]{3,2,1,0:T(8,128)S(1)}, u32[]{:S(2)}, u32[]{:S(2)}) collective-permute-start(f32[2,1,512,128]{3,2,1,0:T(8,128)S(1)} %shard_map.17.near_mine), channel_id=1, source_target_pairs={{0,1},{1,0},{2,3},{3,2},{4,5},{5,4},{6,7},{7,6},{8,9},{9,8},{10,11... | collective-permute-start | bytes 1572872 | tf_op jit(solution)/shard_map/ppermute | solution.py:240
  64.7 0.0 collective-permute-done.11.own_other
  64.7 0.0 collective-permute-done.15.far_other
  64.7 0.0 copy-done.1
  64.7 0.3 shard_map.20.given
  65.1 1.2 %collective-permute-done.5.near_other = f32[2,1,512,128]{3,2,1,0:T(8,128)S(1)} collective-permute-done((f32[2,1,512,128]{3,2,1,0:T(8,128)S(1)}, f32[2,1,512,128]{3,2,1,0:T(8,128)S(1)}, u32[]{:S(2)}, u32[]{:S(2)}) %collective-permute-start.5) | collective-permute-done | bytes 524320 | tf_op jit(solution)/shard_map/ppermute | solution.py:240
  66.2 5.7 %shard_map.21 = (f32[2,512,128]{2,1,0:T(8,128)}, f32[5,256,1024]{2,1,0:T(8,128)S(1)}) custom-call(f32[1,512,128]{2,1,0:T(8,128)S(1)} %collective-permute-done.1.refs_0_.near, f32[2,1,512,128]{3,2,1,0:T(8,128)S(1)} %shard_map.17.near_mine, f32[2,1,512,128]{3,2,1,0:T(8,128)S(1)} %collective-permute-done.5.near_other, ...), custom_call_target="tpu_custom_call", output_to_operand_aliasing={{1}: (3, {})} | custom-call | tf_op jit(solution)/shard_map/pallas_call | solution.py:188
  (5 shorter events, 0.2 us)
Async XLA Ops:
  0.0 64.7 %copy-start.1 = (f32[2,1,256,1,256]{4,3,2,1,0:T(1,128)S(1)}, f32[2,1,256,1,256]{4,3,2,1,0:T(1,128)}, u32[]{:S(2)}) copy-start(f32[2,1,256,1,256]{4,3,2,1,0:T(1,128)} %param.1) | copy-start | bytes 1572868
  1.2 8.0 %collective-permute-start.6 = (f32[1,512,128]{2,1,0:T(8,128)S(1)}, f32[1,512,128]{2,1,0:T(8,128)S(1)}, u32[]{:S(2)}, u32[]{:S(2)}) collective-permute-start(f32[1,512,128]{2,1,0:T(8,128)S(1)} %bitcast.7), channel_id=1, source_target_pairs={{16,0},{17,1},{18,2},{19,3},{20,4},{21,5},{22,6},{23,7}} | collective-permute-start | bytes 786440 | tf_op jit(solution)/shard_map/ppermute | solution.py:252
  3.2 9.9 %collective-permute-start = (f32[1,512,128]{2,1,0:T(8,128)S(1)}, f32[1,512,128]{2,1,0:T(8,128)S(1)}, u32[]{:S(2)}, u32[]{:S(2)}) collective-permute-start(f32[1,512,128]{2,1,0:T(8,128)S(1)} %bitcast.8), channel_id=1, source_target_pairs={{0,8},{8,16},{16,24},{1,9},{9,17},{17,25},{2,10},{10,18},{18,26},{... | collective-permute-start | bytes 786440 | tf_op jit(solution)/shard_map/ppermute | solution.py:252
  5.1 8.4 %collective-permute-start.7 = (f32[1,512,128]{2,1,0:T(8,128)S(1)}, f32[1,512,128]{2,1,0:T(8,128)S(1)}, u32[]{:S(2)}, u32[]{:S(2)}) collective-permute-start(f32[1,512,128]{2,1,0:T(8,128)S(1)} %bitcast.9), channel_id=1, source_target_pairs={{0,24},{8,0},{16,8},{1,25},{9,1},{17,9},{2,26},{10,2},{18,10},{3,2... | collective-permute-start | bytes 786440 | tf_op jit(solution)/shard_map/ppermute | solution.py:252
  8.5 7.1 %collective-permute-start.9 = (f32[2,512,128]{2,1,0:T(8,128)}, f32[2,512,128]{2,1,0:T(8,128)S(1)}, u32[]{:S(2)}, u32[]{:S(2)}) collective-permute-start(f32[2,512,128]{2,1,0:T(8,128)} %bitcast.3), channel_id=1, source_target_pairs={{0,4},{1,3},{2,6},{8,12},{9,11},{10,14},{16,20},{17,19},{18,22},{2... | collective-permute-start | bytes 1572872 | tf_op jit(solution)/shard_map/ppermute | solution.py:230
  13.6 4.0 %collective-permute-start.13 = (f32[2,512,128]{2,1,0:T(8,128)S(1)}, f32[2,512,128]{2,1,0:T(8,128)S(1)}, u32[]{:S(2)}, u32[]{:S(2)}) collective-permute-start(f32[2,512,128]{2,1,0:T(8,128)S(1)} %pad_maximum_fusion.refs_0_.far), channel_id=1, source_target_pairs={{0,4},{1,3},{2,6},{8,12},{9,11},{10,14},{16,20},{17,19},{18,22},{2... | collective-permute-start | bytes 1572872 | tf_op jit(solution)/shard_map/ppermute | solution.py:230
  14.3 14.2 %collective-permute-start.8 = (f32[2,512,128]{2,1,0:T(8,128)}, f32[2,512,128]{2,1,0:T(8,128)S(1)}, u32[]{:S(2)}, u32[]{:S(2)}) collective-permute-start(f32[2,512,128]{2,1,0:T(8,128)} %bitcast.4), channel_id=1, source_target_pairs={{0,2},{1,5},{2,0},{8,10},{9,13},{10,8},{16,18},{17,21},{18,16},{24... | collective-permute-start | bytes 1572872 | tf_op jit(solution)/shard_map/ppermute | solution.py:230
  15.6 12.9 %collective-permute-start.10 = (f32[2,512,128]{2,1,0:T(8,128)S(1)}, f32[2,512,128]{2,1,0:T(8,128)S(1)}, u32[]{:S(2)}, u32[]{:S(2)}) collective-permute-start(f32[2,512,128]{2,1,0:T(8,128)S(1)} %collective-permute-done.9.refs_2_), channel_id=1, source_target_pairs={{4,6},{3,7},{6,4},{12,14},{11,15},{14,12},{20,22},{19,23},{22,20},... | collective-permute-start | bytes 1572872 | tf_op jit(solution)/shard_map/ppermute | solution.py:230
  16.3 34.1 %collective-permute-start.12 = (f32[2,512,128]{2,1,0:T(8,128)S(1)}, f32[2,512,128]{2,1,0:T(8,128)S(1)}, u32[]{:S(2)}, u32[]{:S(2)}) collective-permute-start(f32[2,512,128]{2,1,0:T(8,128)S(1)} %pad_maximum_fusion.refs_0_.far), channel_id=1, source_target_pairs={{0,2},{1,5},{2,0},{8,10},{9,13},{10,8},{16,18},{17,21},{18,16},{24... | collective-permute-start | bytes 1572872 | tf_op jit(solution)/shard_map/ppermute | solution.py:230
  17.6 32.8 %collective-permute-start.14 = (f32[2,512,128]{2,1,0:T(8,128)S(1)}, f32[2,512,128]{2,1,0:T(8,128)S(1)}, u32[]{:S(2)}, u32[]{:S(2)}) collective-permute-start(f32[2,512,128]{2,1,0:T(8,128)S(1)} %collective-permute-done.13.refs_2_), channel_id=1, source_target_pairs={{4,6},{3,7},{6,4},{12,14},{11,15},{14,12},{20,22},{19,23},{22,20},... | collective-permute-start | bytes 1572872 | tf_op jit(solution)/shard_map/ppermute | solution.py:230
  18.3 9.4 %collective-permute-start.1 = (f32[1,512,128]{2,1,0:T(8,128)S(1)}, f32[1,512,128]{2,1,0:T(8,128)S(1)}, u32[]{:S(2)}, u32[]{:S(2)}) collective-permute-start(f32[1,512,128]{2,1,0:T(8,128)S(1)} %collective-permute-done), channel_id=1, source_target_pairs={{8,16},{16,24},{9,17},{17,25},{10,18},{18,26},{11,19},{19,27},{12,... | collective-permute-start | bytes 786440 | tf_op jit(solution)/shard_map/ppermute | solution.py:252
  27.7 24.2 %collective-permute-start.3 = (f32[1,512,128]{2,1,0:T(8,128)S(1)}, f32[1,512,128]{2,1,0:T(8,128)S(1)}, u32[]{:S(2)}, u32[]{:S(2)}) collective-permute-start(f32[1,512,128]{2,1,0:T(8,128)S(1)} %collective-permute-done.1.refs_0_.near), channel_id=1, source_target_pairs={{16,20},{17,19},{18,22},{24,28},{25,27},{26,30}} | collective-permute-start | bytes 786440 | tf_op jit(solution)/shard_map/ppermute | solution.py:230
  28.5 1.0 %copy-start = (f32[2,1,256,1,256]{4,3,2,1,0:T(1,128)S(1)}, f32[2,1,256,1,256]{4,3,2,1,0:T(1,128)}, u32[]{:S(2)}) copy-start(f32[2,1,256,1,256]{4,3,2,1,0:T(1,128)} %param.1) | copy-start | bytes 1572868
  29.6 35.1 %collective-permute-start.11 = (f32[2,2,512,128]{3,2,1,0:T(8,128)S(1)}, f32[2,2,512,128]{3,2,1,0:T(8,128)S(1)}, u32[]{:S(2)}, u32[]{:S(2)}) collective-permute-start(f32[2,2,512,128]{3,2,1,0:T(8,128)S(1)} %shard_map.18.own_mine), channel_id=1, source_target_pairs={{0,1},{1,0},{2,3},{3,2},{4,5},{5,4},{6,7},{7,6},{8,9},{9,8},{10,11... | collective-permute-start | bytes 3145736 | tf_op jit(solution)/shard_map/ppermute | solution.py:240
  50.4 14.3 %collective-permute-start.15 = (f32[2,2,512,128]{3,2,1,0:T(8,128)S(1)}, f32[2,2,512,128]{3,2,1,0:T(8,128)S(1)}, u32[]{:S(2)}, u32[]{:S(2)}) collective-permute-start(f32[2,2,512,128]{3,2,1,0:T(8,128)S(1)} %shard_map.19.far_mine), channel_id=1, source_target_pairs={{0,1},{1,0},{2,3},{3,2},{4,5},{5,4},{6,7},{7,6},{8,9},{9,8},{10,11... | collective-permute-start | bytes 3145736 | tf_op jit(solution)/shard_map/ppermute | solution.py:240
  50.6 7.6 %collective-permute-start.2 = (f32[1,512,128]{2,1,0:T(8,128)S(1)}, f32[1,512,128]{2,1,0:T(8,128)S(1)}, u32[]{:S(2)}, u32[]{:S(2)}) collective-permute-start(f32[1,512,128]{2,1,0:T(8,128)S(1)} %collective-permute-done.1.refs_0_.near), channel_id=1, source_target_pairs={{16,18},{17,21},{18,16},{24,26},{25,29},{26,24}} | collective-permute-start | bytes 786440 | tf_op jit(solution)/shard_map/ppermute | solution.py:230
  51.9 6.3 %collective-permute-start.4 = (f32[1,512,128]{2,1,0:T(8,128)S(1)}, f32[1,512,128]{2,1,0:T(8,128)S(1)}, u32[]{:S(2)}, u32[]{:S(2)}) collective-permute-start(f32[1,512,128]{2,1,0:T(8,128)S(1)} %collective-permute-done.3.refs_2_), channel_id=1, source_target_pairs={{20,22},{19,23},{22,20},{28,30},{27,31},{30,28}} | collective-permute-start | bytes 786440 | tf_op jit(solution)/shard_map/ppermute | solution.py:230
  58.3 8.0 %collective-permute-start.5 = (f32[2,1,512,128]{3,2,1,0:T(8,128)S(1)}, f32[2,1,512,128]{3,2,1,0:T(8,128)S(1)}, u32[]{:S(2)}, u32[]{:S(2)}) collective-permute-start(f32[2,1,512,128]{3,2,1,0:T(8,128)S(1)} %shard_map.17.near_mine), channel_id=1, source_target_pairs={{0,1},{1,0},{2,3},{3,2},{4,5},{5,4},{6,7},{7,6},{8,9},{9,8},{10,11... | collective-permute-start | bytes 1572872 | tf_op jit(solution)/shard_map/ppermute | solution.py:240
